TPU v7x, 32 devices: a whole 2x2x4 slice. The times are simulated.
32 devices in a mesh: dp: 4 (over z), expert: 8 (over y, x, core).
Axes of the slice: x: 2, y: 2, z: 4, core: 2. Of those that a mesh axis runs over, the one named last changes fastest.
Arguments:
- tokens: bfloat16 [8192, 1536], P(('dp', 'expert')), may hold values from -6 to 6
- segment_ids: int32 [8192], P('dp'), may hold values from 0 to 7, never falling along the last dimension, each value on 1 to 2048 neighbouring positions
- expert_ids: int32 [8192, 8], P(('dp', 'expert')), may hold values from 0 to 15, all different within a row; in each aligned block of 256 rows (0 to 255, 256 to 511, ...) at most 160 rows name the same one
- w_query: bfloat16 [1536, 1536], P(('dp', 'expert')), may hold values from -0.5 to 0.5
- w_key_value: bfloat16 [1536, 1024], P(('dp', 'expert')), may hold values from -0.5 to 0.5
- w_out: bfloat16 [1536, 1536], P(None, ('dp', 'expert')), may hold values from -1.75 to 1.75
- w_router: bfloat16 [1536, 16], P(('dp', 'expert')), may hold values from -0.078125 to 0.078125
- norm_attn: bfloat16 [1536], P(('dp', 'expert')), may hold values from 0.5 to 1.5
- norm_moe: bfloat16 [1536], P(('dp', 'expert')), may hold values from 0.5 to 1.5
- w_gate_up: bfloat16 [16, 1536, 1024], P('expert'), may hold values from -0.15625 to 0.15625
- w_down: bfloat16 [16, 512, 1536], P('expert'), may hold values from -6 to 6
- grad_out: bfloat16 [8192, 1536], P(('dp', 'expert')), may hold values from -6 to 6
Outputs:
- result: bfloat16 [8192, 1536], P(('dp', 'expert'))
- grad_tokens: bfloat16 [8192, 1536], P(('dp', 'expert'))
- grad_w_query: float32 [1536, 1536], P(('dp', 'expert'))
- grad_w_key_value: float32 [1536, 1024], P(('dp', 'expert'))
- grad_w_out: float32 [1536, 1536], P(None, ('dp', 'expert'))
- grad_w_router: float32 [1536, 16], P(('dp', 'expert'))
- grad_norm_attn: float32 [1536], P(('dp', 'expert'))
- grad_norm_moe: float32 [1536], P(('dp', 'expert'))
- grad_w_gate_up: float32 [16, 1536, 1024], P('expert', 'dp')
- grad_w_down: float32 [16, 512, 1536], P('expert', None, 'dp')
Inputs may be any that keep to these rules, and one draw needn't show every extreme that they name: `expert_ids`: within the 256 tokens of one device a row names 8 different experts, and no expert is named more than 160 times; in every draw some expert is named exactly 160 times by one device's tokens.
All inputs are finite; a program needn't handle non-finite values.
Results may differ from a plain program's by a relative error of at most 0.02.
Values may be sent and summed in bfloat16 or wider, within the bound.
No kernel may reach another device: no remote copies, remote signals or barrier semaphores. Data moves between devices by JAX's collectives and lax.ppermute only.
A program may use at most 256 MiB of HBM per device.

v0:
```python
import functools

import jax
import jax.numpy as jnp
from jax import lax
from jax.experimental import pallas as pl
from jax.experimental.pallas import tpu as pltpu
from jax.sharding import PartitionSpec as P

D = 1536
HEADS = 24
KV_HEADS = 8
HEAD_DIM = 64
FF = 512
TOP = 8
EXP_DEV = 2

RESIDUAL = 0.22
ATTN_SCALE = 0.015625
LOG2E = 1.4426950408889634
EPSILON = 1e-06
ROPE_BASE = 10000.0
MASKED = -1e30

GROUP = HEADS // KV_HEADS
HALF = HEAD_DIM // 2
BLK = 256
BF = jnp.bfloat16
F32 = jnp.float32
BOTH = ("dp", "expert")


def dot(a, b, ca, cb):
    return lax.dot_general(a, b, (((ca,), (cb,)), ((), ())), preferred_element_type=F32)


def rms_scale(values, gain_vec):
    return (
        values * lax.rsqrt(jnp.mean(values * values, axis=-1, keepdims=True) + EPSILON) * gain_vec
    )


def side_by_side(block):
    return jnp.concatenate(
        [block[h * HEAD_DIM : (h + 1) * HEAD_DIM] for h in range(GROUP)], axis=1
    )


def stacked(wide):
    width = wide.shape[1] // GROUP
    return jnp.concatenate([wide[:, h * width : (h + 1) * width] for h in range(GROUP)], axis=0)


def allowed_keys(start_ref, block, key_block):
    lane = lax.broadcasted_iota(jnp.int32, (1, BLK), 1) + block * BLK
    reach = lane - start_ref[...]
    lane3 = jnp.concatenate([lane] * GROUP, axis=1)
    reach3 = jnp.concatenate([reach] * GROUP, axis=1)
    key_pos = lax.broadcasted_iota(jnp.int32, (BLK, 1), 0) + key_block * BLK
    back = lane3 - key_pos
    return (back >= 0) & (back <= reach3)


def attn_fwd_kernel(first_ref, q_ref, k_ref, vt_ref, start_ref, a_ref, o_ref, lse_ref):
    block = pl.program_id(0)
    query = side_by_side(q_ref[...])
    width = GROUP * BLK

    def step(key_block, carry):
        largest, total, acc = carry
        keys = k_ref[pl.ds(pl.multiple_of(key_block * BLK, BLK), BLK), :]
        values = vt_ref[:, pl.ds(pl.multiple_of(key_block * BLK, BLK), BLK)]
        scores = dot(keys, query, 1, 0) * (ATTN_SCALE * LOG2E)
        scores = jnp.where(allowed_keys(start_ref, block, key_block), scores, MASKED)
        now = jnp.maximum(largest, jnp.max(scores, axis=0, keepdims=True))
        power = jnp.exp2(scores - now)
        fade = jnp.exp2(largest - now)
        total = total * fade + jnp.sum(power, axis=0, keepdims=True)
        acc = acc * fade + dot(values, power.astype(BF), 1, 0)
        return now, total, acc

    largest, total, acc = lax.fori_loop(
        first_ref[block],
        block + 1,
        step,
        (
            jnp.full((1, width), MASKED, F32),
            jnp.zeros((1, width), F32),
            jnp.zeros((HEAD_DIM, width), F32),
        ),
    )
    out = stacked(acc / total)
    o_ref[...] = out
    a_ref[...] = out.astype(BF)
    lse = largest + jnp.log2(total)
    lse_ref[...] = jnp.concatenate(
        [lse[:, h * BLK : (h + 1) * BLK] for h in range(GROUP)]
        + [jnp.zeros((8 - GROUP, BLK), F32)],
        axis=0,
    )


def attn_bwd_kernel(
    first_ref, q_ref, da_ref, o_ref, lse_ref, k_ref, kt_ref, v_ref, start_ref,
    dq_ref, dk_ref, dv_ref, dk_acc, dv_acc,
):
    block = pl.program_id(0)

    @pl.when(block == 0)
    def _():
        dk_acc[...] = jnp.zeros_like(dk_acc)
        dv_acc[...] = jnp.zeros_like(dv_acc)

    query_t = side_by_side(q_ref[...])
    query = query_t.astype(F32).T.astype(BF)
    grad_t = side_by_side(da_ref[0])
    grad_f = grad_t.astype(F32)
    grad = grad_f.T.astype(BF)
    delta = jnp.sum(side_by_side(o_ref[...]) * grad_f, axis=0, keepdims=True)
    lse = jnp.concatenate([lse_ref[h : h + 1, :] for h in range(GROUP)], axis=1)

    def step(key_block, dq):
        rows = pl.ds(pl.multiple_of(key_block * BLK, BLK), BLK)
        keys = k_ref[rows, :]
        scores = dot(keys, query_t, 1, 0) * (ATTN_SCALE * LOG2E)
        scores = jnp.where(allowed_keys(start_ref, block, key_block), scores, MASKED)
        prob = jnp.exp2(scores - lse)
        grad_prob = dot(v_ref[rows, :], grad_t, 1, 0)
        grad_score = (prob * (grad_prob - delta) * ATTN_SCALE).astype(BF)
        dv_acc[rows, :] += dot(prob.astype(BF), grad, 1, 0)
        dk_acc[rows, :] += dot(grad_score, query, 1, 0)
        return dq + dot(kt_ref[:, rows], grad_score, 1, 0)

    dq = lax.fori_loop(
        first_ref[block], block + 1, step, jnp.zeros((HEAD_DIM, GROUP * BLK), F32)
    )
    dq_ref[...] = stacked(dq)

    @pl.when(block == pl.num_programs(0) - 1)
    def _():
        dk_ref[...] = dk_acc[...].T
        dv_ref[...] = dv_acc[...].T


def attn_forward(first, q_t, k, v_t, start):
    seq = q_t.shape[1]
    rows = GROUP * HEAD_DIM
    column = lambda g, first: (0, g)
    whole = lambda g, first: (0, 0)
    return pl.pallas_call(
        attn_fwd_kernel,
        grid_spec=pltpu.PrefetchScalarGridSpec(
            num_scalar_prefetch=1,
            grid=(seq // BLK,),
            in_specs=[
                pl.BlockSpec((rows, BLK), column),
                pl.BlockSpec((seq, HEAD_DIM), whole),
                pl.BlockSpec((HEAD_DIM, seq), whole),
                pl.BlockSpec((1, BLK), column),
            ],
            out_specs=[
                pl.BlockSpec((rows, BLK), column),
                pl.BlockSpec((rows, BLK), column),
                pl.BlockSpec((8, BLK), column),
            ],
        ),
        out_shape=[
            jax.ShapeDtypeStruct((rows, seq), BF),
            jax.ShapeDtypeStruct((rows, seq), F32),
            jax.ShapeDtypeStruct((8, seq), F32),
        ],
        cost_estimate=pl.CostEstimate(
            flops=4 * rows * seq * seq, bytes_accessed=8 * rows * seq, transcendentals=GROUP * seq * seq
        ),
        name="attn_fwd",
    )(first, q_t, k, v_t, start)


def attn_backward(first, q_t, da, o_t, lse, k, k_t, v, start):
    seq = q_t.shape[1]
    rows = GROUP * HEAD_DIM
    column = lambda g, first: (0, g)
    whole = lambda g, first: (0, 0)
    return pl.pallas_call(
        attn_bwd_kernel,
        grid_spec=pltpu.PrefetchScalarGridSpec(
            num_scalar_prefetch=1,
            grid=(seq // BLK,),
            in_specs=[
                pl.BlockSpec((rows, BLK), column),
                pl.BlockSpec((1, rows, BLK), lambda g, first: (g, 0, 0)),
                pl.BlockSpec((rows, BLK), column),
                pl.BlockSpec((8, BLK), column),
                pl.BlockSpec((seq, HEAD_DIM), whole),
                pl.BlockSpec((HEAD_DIM, seq), whole),
                pl.BlockSpec((seq, HEAD_DIM), whole),
                pl.BlockSpec((1, BLK), column),
            ],
            out_specs=[
                pl.BlockSpec((rows, BLK), column),
                pl.BlockSpec((HEAD_DIM, seq), whole),
                pl.BlockSpec((HEAD_DIM, seq), whole),
            ],
            scratch_shapes=[
                pltpu.VMEM((seq, HEAD_DIM), F32),
                pltpu.VMEM((seq, HEAD_DIM), F32),
            ],
        ),
        out_shape=[
            jax.ShapeDtypeStruct((rows, seq), F32),
            jax.ShapeDtypeStruct((HEAD_DIM, seq), F32),
            jax.ShapeDtypeStruct((HEAD_DIM, seq), F32),
        ],
        cost_estimate=pl.CostEstimate(
            flops=10 * rows * seq * seq, bytes_accessed=12 * rows * seq, transcendentals=GROUP * seq * seq
        ),
        name="attn_bwd",
    )(first, q_t, da, o_t, lse, k, k_t, v, start)


PACK = 384
Q_COLS = GROUP * HEAD_DIM
QKV = Q_COLS + 2 * HEAD_DIM
ROUTE = QKV - 256


def spec(shape, index):
    return pl.BlockSpec(shape, index)


def resident(shape):
    return pl.BlockSpec(
        shape, lambda *_: (0,) * len(shape), pipeline_mode=pl.Buffered(1)
    )


def call(kernel, name, grid, in_specs, out_specs, out_shape, flops, moved, scratch=()):
    return pl.pallas_call(
        kernel,
        grid_spec=pltpu.PrefetchScalarGridSpec(
            num_scalar_prefetch=1,
            grid=grid,
            in_specs=in_specs,
            out_specs=out_specs,
            scratch_shapes=list(scratch),
        ),
        out_shape=out_shape,
        cost_estimate=pl.CostEstimate(flops=flops, bytes_accessed=moved, transcendentals=0),
        name=name,
    )


def shape(dims, kind):
    return jax.ShapeDtypeStruct(dims, kind)


def relative(step, half):
    return jnp.where(step < half, 2 * step + 1, 2 * (step - half))


def owner(step, half, pos):
    return relative(step, half) ^ pos[0]


def give_index(step, half):
    return jnp.minimum(step, half - 1)


def keep_index(step, half):
    return jnp.maximum(step - half, 0)


def turn_rows(rows_t, cosine, sine):
    out = []
    for h in range(rows_t.shape[0] // HEAD_DIM):
        a = rows_t[h * HEAD_DIM : h * HEAD_DIM + HALF]
        b = rows_t[h * HEAD_DIM + HALF : (h + 1) * HEAD_DIM]
        out += [a * cosine - b * sine, b * cosine + a * sine]
    return jnp.concatenate(out, axis=0)


def norm_of(values):
    return values * lax.rsqrt(jnp.mean(values * values, axis=1, keepdims=True) + EPSILON)


def qkv_kernel(count, pos_ref, *refs):
    pieces = refs[: count + 2]
    w_ref, gain_ref, cos_ref, sin_ref, q_ref, kt_ref, vt_ref, k_ref, v_ref = refs[count + 2 :]
    gain = gain_ref[...]
    for r in range(count):
        if r < count - 2:
            rows = pieces[r][...]
        else:
            at = count - 2 + 2 * (r - count + 2)
            rows = jnp.concatenate([pieces[at][...], pieces[at + 1][...]], axis=0)
        normed = (norm_of(rows.astype(F32)) * gain).astype(BF)
        both = dot(normed, w_ref[...], 1, 0)
        turned = both.T
        place = pl.multiple_of((pos_ref[0] ^ r) * BLK, BLK)
        columns = pl.ds(place, BLK)
        cosine, sine = cos_ref[:, columns], sin_ref[:, columns]
        qk = turn_rows(turned[: Q_COLS + HEAD_DIM], cosine, sine)
        q_ref[:, columns] = qk[:Q_COLS].astype(BF)
        kt_ref[:, columns] = qk[Q_COLS:].astype(BF)
        vt_ref[:, columns] = turned[Q_COLS + HEAD_DIM : QKV].astype(BF)
        k_ref[columns, :] = qk[Q_COLS:].T.astype(BF)
        v_ref[columns, :] = both[:, 256 : 256 + HEAD_DIM].astype(BF)


def qkv_forward(pos, pieces, weights, gain, cosine, sine):
    count = len(pieces) - 2
    seq = cosine.shape[1]
    full = lambda a: resident(a.shape)
    return call(
        functools.partial(qkv_kernel, count),
        "qkv",
        (1,),
        [full(a) for a in pieces] + [full(a) for a in (weights, gain, cosine, sine)],
        [resident(s) for s in ((Q_COLS, seq), (HEAD_DIM, seq), (HEAD_DIM, seq), (seq, HEAD_DIM), (seq, HEAD_DIM))],
        [
            shape((Q_COLS, seq), BF),
            shape((HEAD_DIM, seq), BF),
            shape((HEAD_DIM, seq), BF),
            shape((seq, HEAD_DIM), BF),
            shape((seq, HEAD_DIM), BF),
        ],
        2 * seq * D * PACK,
        2 * seq * D,
    )(pos, *pieces, weights, gain, cosine, sine)


def mix_kernel(count, pos_ref, *refs):
    pieces = refs[: count + 2]
    x_ref, w_ref, gain_ref, route_ref, ids_ref = refs[count + 2 : count + 7]
    h2_ref, gates_ref, y1_ref, h2_own_ref, gates_own_ref, heads = refs[count + 7 :]
    block = pl.program_id(0)
    pos = pos_ref[0]
    for r in range(count):
        base = (pos ^ r) * Q_COLS
        if r < count - 2:
            heads[pl.ds(pl.multiple_of(base, Q_COLS), Q_COLS), :] = pieces[r][...]
        else:
            half = Q_COLS // 2
            at = count - 2 + 2 * (r - count + 2)
            heads[pl.ds(pl.multiple_of(base, half), half), :] = pieces[at][...]
            heads[pl.ds(pl.multiple_of(base + half, half), half), :] = pieces[at + 1][...]
    y1 = x_ref[0].astype(F32) + RESIDUAL * dot(heads[...], w_ref[...], 0, 0)
    h2 = (norm_of(y1) * gain_ref[...]).astype(BF)
    logits = dot(h2, route_ref[...], 1, 0)
    lane = lax.broadcasted_iota(jnp.int32, logits.shape, 1) - ROUTE
    ids = ids_ref[...]
    chosen = lane == ids[:, 0:1]
    for k in range(1, TOP):
        chosen = chosen | (lane == ids[:, k : k + 1])
    masked = jnp.where(chosen, logits, MASKED)
    power = jnp.where(chosen, jnp.exp(masked - jnp.max(masked, axis=1, keepdims=True)), 0.0)
    gates = power / jnp.sum(power, axis=1, keepdims=True)
    h2_ref[...] = h2
    gates_ref[...] = gates

    @pl.when(block == pos)
    def _():
        y1_ref[...] = y1
        h2_own_ref[...] = h2
        gates_own_ref[...] = gates


def mix_forward(pos, pieces, x_rel, w_full, gain, weights, ids):
    count = len(pieces) - 2
    seq = ids.shape[0]
    row = lambda s, pos: (s, 0)
    return call(
        functools.partial(mix_kernel, count),
        "mix",
        (seq // BLK,),
        [spec((a.shape[0], BLK), lambda s, pos: (0, s)) for a in pieces]
        + [
            spec((1, BLK, D), lambda s, pos: (s ^ pos[0], 0, 0)),
            resident(w_full.shape),
            resident(gain.shape),
            pl.BlockSpec((D, 128), lambda s, pos: (0, 2), pipeline_mode=pl.Buffered(1)),
            spec((BLK, TOP), row),
        ],
        [
            spec((BLK, D), row),
            spec((BLK, 128), row),
            resident((BLK, D)),
            resident((BLK, D)),
            resident((BLK, 128)),
        ],
        [
            shape((seq, D), BF),
            shape((seq, 128), F32),
            shape((BLK, D), F32),
            shape((BLK, D), BF),
            shape((BLK, 128), F32),
        ],
        2 * seq * D * D,
        10 * seq * D,
        [pltpu.VMEM((HEADS * HEAD_DIM, BLK), BF)],
    )(pos, *pieces, x_rel, w_full, gain, weights, ids)


def expert_kernel(
    half, pos_ref, h2_ref, dy_ref, gates_ref, up_ref, down_ref,
    give_ref, keep_ref, ag_ref, dgu_ref, dg_ref,
):
    step = pl.program_id(0)
    h2, dy, gates = h2_ref[...], dy_ref[...], gates_ref[...]
    lane = lax.broadcasted_iota(jnp.int32, gates.shape, 1) - ROUTE - EXP_DEV * pos_ref[0]
    total = None
    gate_grads = jnp.zeros(gates.shape, F32)
    for e in range(EXP_DEV):
        gate = RESIDUAL * jnp.sum(jnp.where(lane == e, gates, 0.0), axis=1, keepdims=True)
        gu = dot(h2, up_ref[e], 1, 0)
        back = dot(dy, down_ref[e], 1, 1)
        g, u = gu[:, :FF], gu[:, FF:]
        sig = 1.0 / (1.0 + jnp.exp(-g))
        swish = g * sig
        act = swish * u
        gate_grad = RESIDUAL * jnp.sum(act * back, axis=1, keepdims=True)
        which = lax.broadcasted_iota(jnp.int32, gates.shape, 1)
        gate_grads = jnp.where(which == e, gate_grad, gate_grads)
        ag_ref[e] = (gate * act).astype(BF)
        dact = gate * back
        dgu = jnp.concatenate(
            [dact * u * (sig * (1.0 + g * (1.0 - sig))), dact * swish], axis=1
        ).astype(BF)
        dgu_ref[e] = dgu
        term = dot(dgu, up_ref[e], 1, 1)
        total = term if total is None else total + term
    dg_ref[0] = gate_grads.T[:8]

    @pl.when(step < half)
    def _():
        give_ref[0] = total.astype(BF)

    @pl.when(step >= half)
    def _():
        keep_ref[0] = total.astype(BF)


def expert_main(pos, h2, dy_all, gates, w_gate_up, w_down):
    seq = h2.shape[0]
    steps = seq // BLK
    half = steps // 2
    row = lambda s, pos: (owner(s, half, pos), 0)
    each = lambda s, pos: (0, owner(s, half, pos), 0)
    return call(
        functools.partial(expert_kernel, half),
        "experts",
        (steps,),
        [
            spec((BLK, D), row),
            spec((BLK, D), row),
            spec((BLK, 128), row),
            resident(w_gate_up.shape),
            resident(w_down.shape),
        ],
        [
            spec((1, BLK, D), lambda s, pos: (give_index(s, half), 0, 0)),
            spec((1, BLK, D), lambda s, pos: (keep_index(s, half), 0, 0)),
            spec((EXP_DEV, BLK, FF), each),
            spec((EXP_DEV, BLK, 2 * FF), each),
            spec((1, 8, BLK), lambda s, pos: (owner(s, half, pos), 0, 0)),
        ],
        [
            shape((half, BLK, D), BF),
            shape((half, BLK, D), BF),
            shape((EXP_DEV, seq, FF), BF),
            shape((EXP_DEV, seq, 2 * FF), BF),
            shape((steps, 8, BLK), F32),
        ],
        10 * EXP_DEV * seq * D * FF,
        20 * seq * D,
    )(pos, h2, dy_all, gates, w_gate_up, w_down)


def down_grad_kernel(pos_ref, ag_ref, dy_ref, out_ref):
    out_ref[0, 0] = dot(ag_ref[0], dy_ref[...], 0, 0).astype(BF)


def down_grad(pos, ag, dy_all, groups):
    seq = dy_all.shape[0]
    cols = D // groups
    wide = cols if cols % 128 == 0 else D
    out = call(
        down_grad_kernel,
        "down_grad",
        (EXP_DEV, D // wide),
        [
            spec((1, seq, FF), lambda e, s, pos: (e, 0, 0)),
            spec((seq, wide), lambda e, s, pos: (0, s)),
        ],
        spec((1, 1, FF, wide), lambda e, s, pos: (s, e, 0, 0)),
        shape((D // wide, EXP_DEV, FF, wide), BF),
        2 * EXP_DEV * seq * D * FF,
        8 * seq * D,
    )(pos, ag, dy_all)
    if wide == cols:
        return out
    return jnp.moveaxis(out[0].reshape(EXP_DEV, FF, groups, cols), 2, 0)


def up_grad_kernel(pos_ref, h2_ref, dgu_ref, out_ref):
    out_ref[0] = dot(h2_ref[...], dgu_ref[0], 0, 0).astype(BF)


def up_grad(pos, h2, dgu, groups):
    seq = h2.shape[0]
    rows = 384
    out = call(
        up_grad_kernel,
        "up_grad",
        (EXP_DEV, D // rows),
        [
            spec((seq, rows), lambda e, s, pos: (0, s)),
            spec((1, seq, 2 * FF), lambda e, s, pos: (e, 0, 0)),
        ],
        spec((1, rows, 2 * FF), lambda e, s, pos: (e, s, 0)),
        shape((EXP_DEV, D, 2 * FF), BF),
        4 * EXP_DEV * seq * D * FF,
        8 * seq * D,
    )(pos, h2, dgu)
    return out


def combine_kernel(half, pos_ref, ag_ref, down_ref, give_ref, keep_ref):
    step = pl.program_id(0)
    total = dot(ag_ref[0], down_ref[0], 1, 0)
    for e in range(1, EXP_DEV):
        total = total + dot(ag_ref[e], down_ref[e], 1, 0)

    @pl.when(step < half)
    def _():
        give_ref[0] = total.astype(BF)

    @pl.when(step >= half)
    def _():
        keep_ref[0] = total.astype(BF)


def combine(pos, ag, w_down):
    seq = ag.shape[1]
    steps = seq // BLK
    half = steps // 2
    return call(
        functools.partial(combine_kernel, half),
        "combine",
        (steps,),
        [
            spec((EXP_DEV, BLK, FF), lambda s, pos: (0, owner(s, half, pos), 0)),
            resident(w_down.shape),
        ],
        [
            spec((1, BLK, D), lambda s, pos: (give_index(s, half), 0, 0)),
            spec((1, BLK, D), lambda s, pos: (keep_index(s, half), 0, 0)),
        ],
        [shape((half, BLK, D), BF), shape((half, BLK, D), BF)],
        2 * EXP_DEV * seq * D * FF,
        4 * seq * D,
    )(pos, ag, w_down)


def norm_pull(values, gain, grad):
    scale = lax.rsqrt(jnp.mean(values * values, axis=1, keepdims=True) + EPSILON)
    unit = values * scale
    inner = grad * gain
    pulled = scale * (inner - unit * jnp.mean(inner * unit, axis=1, keepdims=True))
    return pulled, jnp.sum(grad * unit, axis=0, keepdims=True)


def middle_kernel(
    pos_ref, keep_ref, got_ref, fx_ref, fy_ref, y1_ref, h2_ref, gates_ref, dg_ref, dy_ref,
    route_ref, gain_ref, w_ref, dy1_ref, db_ref, da_ref, router_ref, gain_grad_ref,
):
    dh2 = (
        keep_ref[0].astype(F32)
        + got_ref[0].astype(F32)
        + fx_ref[...].astype(F32)
        + fy_ref[...].astype(F32)
    )
    gates, gate_grads = gates_ref[...], dg_ref[...]
    mean = jnp.sum(gates * gate_grads, axis=1, keepdims=True)
    dlogits = (gates * (gate_grads - mean)).astype(BF)
    dh2 = dh2 + dot(dlogits, route_ref[...], 1, 1)
    router_ref[...] = dot(h2_ref[...], dlogits, 0, 0)
    pulled, gain_grad = norm_pull(y1_ref[...], gain_ref[...], dh2)
    gain_grad_ref[...] = jnp.broadcast_to(gain_grad, gain_grad_ref.shape)
    dy1 = dy_ref[...].astype(F32) + pulled
    dy1_ref[...] = dy1
    db = (RESIDUAL * dy1).astype(BF)
    db_ref[...] = db
    da = dot(w_ref[...], db, 1, 1).astype(BF)
    for j in range(da_ref.shape[0]):
        da_ref[j] = da[j * Q_COLS : (j + 1) * Q_COLS]


def middle(pos, keep, got, fx, fy, y1, h2, gates, dg, dy, weights, gain, w_full):
    rows = y1.shape[0]
    full = lambda a: resident(a.shape)
    first = pl.BlockSpec((1, rows, D), lambda s, pos: (0, 0, 0), pipeline_mode=pl.Buffered(1))
    members = HEADS * HEAD_DIM // Q_COLS
    return call(
        middle_kernel,
        "middle",
        (1,),
        [first, first]
        + [full(a) for a in (fx, fy, y1, h2, gates, dg, dy)]
        + [
            pl.BlockSpec((D, 128), lambda s, pos: (0, 2), pipeline_mode=pl.Buffered(1)),
            full(gain),
            full(w_full),
        ],
        [
            resident((rows, D)),
            resident((rows, D)),
            resident((members, Q_COLS, rows)),
            resident((D, 128)),
            resident((8, D)),
        ],
        [
            shape((rows, D), F32),
            shape((rows, D), BF),
            shape((members, Q_COLS, rows), BF),
            shape((D, 128), F32),
            shape((8, D), F32),
        ],
        2 * rows * D * D,
        4 * D * D,
    )(pos, keep, got, fx, fy, y1, h2, gates, dg, dy, weights, gain, w_full)


def back_kernel(
    half, pos_ref, dq_ref, dk_ref, dv_ref, cos_ref, sin_ref, w_ref, give_ref, keep_ref, packed_ref
):
    step = pl.program_id(0)
    cosine, sine = cos_ref[...], -sin_ref[...]
    rows = jnp.concatenate(
        [
            turn_rows(dq_ref[...], cosine, sine),
            turn_rows(dk_ref[...], cosine, sine),
            dv_ref[...],
            jnp.zeros((PACK - QKV, BLK), F32),
        ],
        axis=0,
    ).astype(BF)
    packed_ref[...] = rows
    total = dot(rows, w_ref[...], 0, 1).astype(BF)

    @pl.when(step < half)
    def _():
        give_ref[0] = total

    @pl.when(step >= half)
    def _():
        keep_ref[0] = total


def back(pos, dq_t, dk_t, dv_t, cosine, sine, weights):
    seq = dq_t.shape[1]
    steps = seq // BLK
    half = steps // 2
    column = lambda s, pos: (0, owner(s, half, pos))
    return call(
        functools.partial(back_kernel, half),
        "back",
        (steps,),
        [
            spec((Q_COLS, BLK), column),
            spec((HEAD_DIM, BLK), column),
            spec((HEAD_DIM, BLK), column),
            spec((HALF, BLK), column),
            spec((HALF, BLK), column),
            resident(weights.shape),
        ],
        [
            spec((1, BLK, D), lambda s, pos: (give_index(s, half), 0, 0)),
            spec((1, BLK, D), lambda s, pos: (keep_index(s, half), 0, 0)),
            spec((PACK, BLK), column),
        ],
        [
            shape((half, BLK, D), BF),
            shape((half, BLK, D), BF),
            shape((PACK, seq), BF),
        ],
        2 * seq * D * PACK,
        4 * seq * D,
    )(pos, dq_t, dk_t, dv_t, cosine, sine, weights)


def low_pair(values):
    high = values.astype(BF).astype(F32)
    return high, values - high


def pack_kernel(pos_ref, packed_ref, x_ref, gain_ref, router_ref, moe_ref, out_ref, acc):
    step = pl.program_id(0)

    @pl.when(step == 0)
    def _():
        acc[...] = jnp.zeros_like(acc)

    normed = (norm_of(x_ref[0].astype(F32)) * gain_ref[...]).astype(BF)
    acc[...] += dot(packed_ref[...], normed, 1, 0)

    @pl.when(step == pl.num_programs(0) - 1)
    def _():
        out_ref[:, :256] = acc[:256].T.astype(BF)
        lane = lax.broadcasted_iota(jnp.int32, (D, 128), 1)
        high, low = low_pair(router_ref[...])
        gain_high, gain_low = low_pair(moe_ref[...].T)
        rest = acc[256:].T + high + pltpu.roll(low, 16, 1)
        rest = jnp.where(lane == ROUTE + 32, gain_high[:, :1], rest)
        rest = jnp.where(lane == ROUTE + 33, gain_low[:, :1], rest)
        out_ref[:, 256:] = rest.astype(BF)


def pack(pos, packed, x_rel, gain, router, moe):
    seq = packed.shape[1]
    return call(
        pack_kernel,
        "pack",
        (seq // BLK,),
        [
            spec((PACK, BLK), lambda s, pos: (0, s)),
            spec((1, BLK, D), lambda s, pos: (s ^ pos[0], 0, 0)),
            resident(gain.shape),
            resident(router.shape),
            resident(moe.shape),
        ],
        resident((D, PACK)),
        shape((D, PACK), BF),
        2 * seq * D * PACK,
        4 * seq * D,
        [pltpu.VMEM((PACK, D), F32)],
    )(pos, packed, x_rel, gain, router, moe)


def last_kernel(
    pos_ref, keep_ref, got_ref, fx_ref, fy_ref, x_ref, gain_ref, dy1_ref, out_ref, gain_grad_ref
):
    dh1 = (
        keep_ref[0].astype(F32)
        + got_ref[0].astype(F32)
        + fx_ref[...].astype(F32)
        + fy_ref[...].astype(F32)
    )
    pulled, gain_grad = norm_pull(x_ref[...].astype(F32), gain_ref[...], dh1)
    out_ref[...] = (dy1_ref[...] + pulled).astype(BF)
    gain_grad_ref[...] = jnp.broadcast_to(gain_grad, gain_grad_ref.shape)


def last(pos, keep, got, fx, fy, x, gain, dy1):
    rows = x.shape[0]
    full = lambda a: resident(a.shape)
    first = pl.BlockSpec((1, rows, D), lambda s, pos: (0, 0, 0), pipeline_mode=pl.Buffered(1))
    return call(
        last_kernel,
        "last",
        (1,),
        [first, first] + [full(a) for a in (fx, fy, x, gain, dy1)],
        [resident((rows, D)), resident((8, D))],
        [shape((rows, D), BF), shape((8, D), F32)],
        20 * rows * D,
        14 * rows * D,
    )(pos, keep, got, fx, fy, x, gain, dy1)


def out_grad_kernel(count, pos_ref, *refs):
    pieces = refs[: count + 2]
    db_ref, out_ref, heads = refs[count + 2 :]
    step = pl.program_id(0)
    pos = pos_ref[0]
    for r in range(count):
        base = (pos ^ r) * Q_COLS
        if r < count - 2:
            heads[pl.ds(pl.multiple_of(base, Q_COLS), Q_COLS), :] = pieces[r][...]
        else:
            half = Q_COLS // 2
            at = count - 2 + 2 * (r - count + 2)
            heads[pl.ds(pl.multiple_of(base, half), half), :] = pieces[at][...]
            heads[pl.ds(pl.multiple_of(base + half, half), half), :] = pieces[at + 1][...]
    term = dot(db_ref[...], heads[...], 0, 1)

    @pl.when(step == 0)
    def _():
        out_ref[...] = term

    @pl.when(step > 0)
    def _():
        out_ref[...] += term


def out_grad(pos, pieces, db_cols):
    count = len(pieces) - 2
    seq, cols = db_cols.shape
    return call(
        functools.partial(out_grad_kernel, count),
        "out_grad",
        (seq // BLK,),
        [spec((a.shape[0], BLK), lambda s, pos: (0, s)) for a in pieces]
        + [spec((BLK, cols), lambda s, pos: (s, 0))],
        resident((cols, HEADS * HEAD_DIM)),
        shape((cols, HEADS * HEAD_DIM), F32),
        2 * seq * D * cols,
        4 * seq * D,
        [pltpu.VMEM((HEADS * HEAD_DIM, BLK), BF)],
    )(pos, *pieces, db_cols).astype(BF)


def unpack_kernel(groups, members, pos_ref, came_ref, query_ref, pair_ref, rest_ref):
    total = None
    for j in range(members):
        here = came_ref[j].astype(F32)
        for i in range(1, groups):
            here = here + came_ref[i * members + j].astype(F32)
        query_ref[:, j * Q_COLS : (j + 1) * Q_COLS] = here[:, :Q_COLS]
        pair_ref[:, j * HEAD_DIM : (j + 1) * HEAD_DIM] = here[:, Q_COLS : Q_COLS + HEAD_DIM]
        at = (members + j) * HEAD_DIM
        pair_ref[:, at : at + HEAD_DIM] = here[:, Q_COLS + HEAD_DIM : QKV]
        rest = here[:, 256:]
        total = rest if total is None else total + rest
    rest_ref[...] = total


def unpack(pos, came, groups):
    devices, rows, _ = came.shape
    members = devices // groups
    return call(
        functools.partial(unpack_kernel, groups, members),
        "unpack",
        (1,),
        [resident(came.shape)],
        [resident((rows, D)), resident((rows, 2 * KV_HEADS * HEAD_DIM)), resident((rows, 128))],
        [
            shape((rows, D), F32),
            shape((rows, 2 * KV_HEADS * HEAD_DIM), F32),
            shape((rows, 128), F32),
        ],
        devices * rows * PACK,
        4 * devices * rows * PACK,
    )(pos, came)


def swap(values, bit):
    count = lax.axis_size("expert")
    return lax.ppermute(values, "expert", [(i, i ^ bit) for i in range(count)])


def gather_pieces(own):
    half = own.shape[0] // 2
    x, y = swap(own, 2), swap(own, 4)
    core = swap(own, 1)
    far_a, far_b = swap(x[:half], 4), swap(y[half:], 2)
    return [
        own, core, x, swap(x, 1), y, swap(y, 1),
        far_a, far_b, swap(far_a, 1), swap(far_b, 1),
    ]


def scatter_sum(give, keep):
    half = keep.shape[1] // 2
    got = swap(give, 1)

    def pair(which, low, high):
        return keep[which, low:high].astype(F32) + got[which, low:high].astype(F32)

    far_a = swap(pair(3, 0, half).astype(BF), 2)
    far_b = swap(pair(3, half, 2 * half).astype(BF), 4)
    via_y = jnp.concatenate(
        [pair(2, 0, half) + far_a.astype(F32), pair(2, half, 2 * half)], axis=0
    ).astype(BF)
    via_x = jnp.concatenate(
        [pair(1, 0, half), pair(1, half, 2 * half) + far_b.astype(F32)], axis=0
    ).astype(BF)
    return got, swap(via_x, 2), swap(via_y, 4)


def exchange(blocks, axes):
    return lax.all_to_all(blocks, axes, split_axis=0, concat_axis=0, tiled=True)


def shards(
    tokens,
    segment_ids,
    expert_ids,
    w_query,
    w_key_value,
    w_out,
    w_router,
    norm_attn,
    norm_moe,
    w_gate_up,
    w_down,
    grad_out,
):
    tok_rows = tokens.shape[0]
    members = lax.axis_size("expert")
    groups = lax.axis_size("dp")
    position = lax.axis_index("expert")
    pos = position.astype(jnp.int32).reshape(1)
    devices = groups * members
    seq = tok_rows * members
    expert_total = EXP_DEV * members
    in_rows = w_query.shape[0]
    out_cols = w_out.shape[1]
    kv_cols = KV_HEADS * HEAD_DIM

    x_pieces = gather_pieces(tokens)

    own = jnp.concatenate(
        [
            w_query.reshape(in_rows, members, Q_COLS),
            w_key_value[:, :kv_cols].reshape(in_rows, members, HEAD_DIM),
            w_key_value[:, kv_cols:].reshape(in_rows, members, HEAD_DIM),
            jnp.broadcast_to(
                jnp.concatenate(
                    [
                        w_router,
                        norm_attn[:, None],
                        norm_moe[:, None],
                        jnp.zeros((in_rows, PACK - QKV - expert_total - 2), BF),
                    ],
                    axis=1,
                )[:, None, :],
                (in_rows, members, PACK - QKV),
            ),
        ],
        axis=2,
    )
    own = jnp.moveaxis(own, 1, 0)
    own = jnp.broadcast_to(own[None], (groups,) + own.shape).reshape(devices, in_rows, PACK)
    weights = exchange(own, BOTH).reshape(D, PACK)
    gain_attn = weights[:, QKV + expert_total].astype(F32)[None]
    gain_moe = weights[:, QKV + expert_total + 1].astype(F32)[None]

    ids_t = exchange(
        jnp.broadcast_to(expert_ids.T[None], (members, TOP, tok_rows)), "expert"
    )
    ids = jnp.moveaxis(ids_t.reshape(members, TOP, tok_rows), 1, 2).reshape(seq, TOP)
    w_full = lax.all_gather(w_out.T, BOTH, axis=0, tiled=True).T
    dy_all = lax.all_gather(grad_out, "expert", axis=0, tiled=True)

    token_pos = jnp.arange(seq, dtype=jnp.int32)
    start = jnp.sum(
        (segment_ids[:, None] < segment_ids[None, :]).astype(jnp.int32), axis=0, keepdims=True
    )
    first = start[0, ::BLK] // BLK
    frequency = ROPE_BASE ** (-(jnp.arange(HALF, dtype=F32) * 2.0 / HEAD_DIM))
    angles = frequency[:, None] * token_pos.astype(F32)[None, :]
    cosine, sine = jnp.cos(angles), jnp.sin(angles)

    q_t, k_t, v_t, k, v = qkv_forward(pos, x_pieces, weights, gain_attn, cosine, sine)
    a_t, o_t, lse = attn_forward(first, q_t, k, v_t, start)
    a_pieces = gather_pieces(a_t)
    x_rel = jnp.concatenate(
        [piece for piece in x_pieces], axis=0
    ).reshape(members, tok_rows, D)

    h2, gates, y1, h2_own, gates_own = mix_forward(
        pos, a_pieces, x_rel, w_full, gain_moe, weights, ids
    )

    give, keep, ag, dgu, dg = expert_main(pos, h2, dy_all, gates, w_gate_up, w_down)
    dg = exchange(dg, "expert")[:, :EXP_DEV].reshape(expert_total, tok_rows).T
    dg = jnp.pad(dg, ((0, 0), (ROUTE, 128 - ROUTE - expert_total)))
    got, from_x, from_y = scatter_sum(give, keep)

    down_wgrad = down_grad(pos, ag, dy_all, groups)
    down_share = lax.psum_scatter(
        down_wgrad.reshape(groups * EXP_DEV * FF, -1), "dp", scatter_dimension=0, tiled=True
    ).astype(F32).reshape(EXP_DEV, FF, -1)
    up_wgrad = up_grad(pos, h2, dgu, groups)
    up_share = lax.psum_scatter(up_wgrad, "dp", scatter_dimension=1, tiled=True).astype(F32)

    out_give, out_keep = combine(pos, ag, w_down)
    out_got, out_x, out_y = scatter_sum(out_give, out_keep)
    result = (
        y1
        + out_keep[0].astype(F32)
        + out_got[0].astype(F32)
        + out_x.astype(F32)
        + out_y.astype(F32)
    ).astype(BF)

    dy1, db, da, router_wgrad, moe_gain_grad = middle(
        pos, keep, got, from_x, from_y, y1, h2_own, gates_own, dg, grad_out, weights, gain_moe, w_full
    )
    da = exchange(da, "expert")

    db_cols = exchange(
        jnp.moveaxis(db.reshape(tok_rows, groups, members, out_cols), 2, 0).reshape(
            members, tok_rows, groups * out_cols
        ),
        "expert",
    ).reshape(seq, groups * out_cols)
    out_wgrad = out_grad(pos, a_pieces, db_cols).reshape(groups, out_cols, D)
    out_share = jnp.sum(exchange(out_wgrad, "dp").astype(F32), axis=0).T

    dq_t, dk_t, dv_t = attn_backward(first, q_t, da, o_t, lse, k, k_t, v, start)
    give1, keep1, packed = back(pos, dq_t, dk_t, dv_t, cosine, sine, weights)
    got1, from_x1, from_y1 = scatter_sum(give1, keep1)

    sent = pack(pos, packed, x_rel, gain_attn, router_wgrad, moe_gain_grad)
    came = exchange(sent.reshape(devices, in_rows, PACK), BOTH)
    query_share, pair_share, rest = unpack(pos, came, groups)
    router_share = (
        rest[:, ROUTE : ROUTE + expert_total]
        + rest[:, ROUTE + expert_total : ROUTE + 2 * expert_total]
    )
    moe_gain_share = rest[:, ROUTE + 32] + rest[:, ROUTE + 33]

    token_grad, attn_gain_grad = last(pos, keep1, got1, from_x1, from_y1, tokens, gain_attn, dy1)
    gain_rows = jnp.pad(
        attn_gain_grad[0].reshape(devices, in_rows), ((0, 0), (0, 128 - in_rows))
    )
    attn_gain_share = jnp.sum(exchange(gain_rows, BOTH), axis=0)[:in_rows]

    return (
        result,
        token_grad,
        query_share,
        pair_share,
        out_share,
        router_share,
        attn_gain_share,
        moe_gain_share,
        up_share,
        down_share,
    )


def solution(mesh):
    in_specs = (
        P(("dp", "expert"), None),
        P("dp"),
        P(("dp", "expert"), None),
        P(("dp", "expert"), None),
        P(("dp", "expert"), None),
        P(None, ("dp", "expert")),
        P(("dp", "expert"), None),
        P(("dp", "expert")),
        P(("dp", "expert")),
        P("expert", None, None),
        P("expert", None, None),
        P(("dp", "expert"), None),
    )
    out_specs = (
        P(("dp", "expert"), None),
        P(("dp", "expert"), None),
        P(("dp", "expert"), None),
        P(("dp", "expert"), None),
        P(None, ("dp", "expert")),
        P(("dp", "expert"), None),
        P(("dp", "expert")),
        P(("dp", "expert")),
        P("expert", "dp", None),
        P("expert", None, "dp"),
    )
    return jax.shard_map(shards, mesh=mesh, in_specs=in_specs, out_specs=out_specs, check_vma=False)
```

profile of v0, /device:TPU:0, one launch (start us, length us, event | category | flops | bytes accessed | tf_op | source)
XLA Modules:
  0.0 529.7 jit_solution(12553371492818522369)
XLA Ops:
  21.3 6.3 %all-to-all-start = ((bf16[32,48,384]{2,1,0:T(8,128)(2,1)}), bf16[32,48,384]{2,1,0:T(8,128)(2,1)S(1)}, u32[]{:S(2)}, u32[]{:S(2)}) async-start(bf16[32,48,384]{2,1,0:T(8,128)(2,1)} %bitcast.6), calls=%async_computation | async-start | bytes 2359296 | tf_op jit(solution)/shard_map/all_to_all | solution.py:881
  34.3 27.6 %collective-permute-done.3.refs_4_ = bf16[256,1536]{1,0:T(8,128)(2,1)S(1)} collective-permute-done((bf16[256,1536]{1,0:T(8,128)(2,1)S(1)}, bf16[256,1536]{1,0:T(8,128)(2,1)S(1)}, u32[]{:S(2)}, u32[]{:S(2)}) %collective-permute-start.3) | collective-permute-done | bytes 786464 | tf_op jit(solution)/shard_map/ppermute | solution.py:848
  71.5 8.3 %collective-permute-done.6.refs_7_ = bf16[128,1536]{1,0:T(8,128)(2,1)} collective-permute-done((bf16[128,1536]{1,0:T(8,128)(2,1)}, bf16[128,1536]{1,0:T(8,128)(2,1)}, u32[]{:S(2)}, u32[]{:S(2)}) %collective-permute-start.6) | collective-permute-done | bytes 393248 | tf_op jit(solution)/shard_map/ppermute | solution.py:848
  87.5 9.2 %qkv.1 = (bf16[192,2048]{1,0:T(8,128)(2,1)}, bf16[64,2048]{1,0:T(8,128)(2,1)}, bf16[64,2048]{1,0:T(8,128)(2,1)}, bf16[2048,64]{1,0:T(8,128)(2,1)}, bf16[2048,64]{1,0:T(8,128)(2,1)}) custom-call(s32[1]{0:T(128)} %bitcast.pos_ref, bf16[256,1536]{1,0:T(8,128)(2,1)} %x_ref.1, bf16[256,1536]{1,0:T(8,128)(2,1)} %collective-permute-done.refs_1_, ...), custom_call_target="tpu_custom_call" | custom-call | flops 2415919104 | bytes 6291456 | tf_op jit(solution)/shard_map/qkv/pallas_call | solution.py:314
  96.7 23.2 %attn_fwd.1 = (bf16[192,2048]{1,0:T(8,128)(2,1)}, f32[192,2048]{1,0:T(8,128)}, f32[8,2048]{1,0:T(8,128)}) custom-call(s32[8]{0:T(128)} %and_select_fusion.first_ref, bf16[192,2048]{1,0:T(8,128)(2,1)} %get-tuple-element.46.q_ref, bf16[2048,64]{1,0:T(8,128)(2,1)} %get-tuple-element.47.k_ref, bf16[64,2048]{1,0:T(8,128)(2,1)} %get-tuple-element.48.vt_ref, ...), custom_call_target="tpu_custom_call" | custom-call | flops 3221225472 | bytes 3145728 | tf_op jit(solution)/shard_map/attn_fwd/pallas_call | solution.py:150
  128.3 26.6 %collective-permute-done.12.refs_4_ = bf16[192,2048]{1,0:T(8,128)(2,1)S(1)} collective-permute-done((bf16[192,2048]{1,0:T(8,128)(2,1)}, bf16[192,2048]{1,0:T(8,128)(2,1)S(1)}, u32[]{:S(2)}, u32[]{:S(2)}) %collective-permute-start.12) | collective-permute-done | bytes 786464 | tf_op jit(solution)/shard_map/ppermute | solution.py:848
  171.7 6.7 %copy.57 = bf16[1536,1536]{0,1:T(8,128)(2,1)} copy(bf16[1536,1536]{1,0:T(8,128)(2,1)} %all-gather.3.cloned.1.call-done) | data formatting | bytes 9437184 | tf_op jit(solution)/shard_map/all_gather | solution.py:942
  179.3 23.1 %mix.1 = (bf16[2048,1536]{1,0:T(8,128)(2,1)}, f32[2048,128]{1,0:T(8,128)}, f32[256,1536]{1,0:T(8,128)}, bf16[256,1536]{1,0:T(8,128)(2,1)}, f32[256,128]{1,0:T(8,128)}) custom-call(s32[1]{0:T(128)} %bitcast.pos_ref, bf16[192,2048]{1,0:T(8,128)(2,1)} %get-tuple-element.49.refs_0_, bf16[192,2048]{1,0:T(8,128)(2,1)} %copy-done.16, bf16[192,2048]{1,0:T(8,128)(2,1)} %copy-done.6, ...), custom_call_target="tpu_custom_call" | custom-call | flops 9663676416 | bytes 31457280 | tf_op jit(solution)/shard_map/mix/pallas_call | solution.py:372
  202.4 44.8 %experts.1 = (bf16[4,256,1536]{2,1,0:T(8,128)(2,1)}, bf16[4,256,1536]{2,1,0:T(8,128)(2,1)}, bf16[2,2048,512]{2,1,0:T(8,128)(2,1)}, bf16[2,2048,1024]{2,1,0:T(8,128)(2,1)}, f32[8,8,256]{2,1,0:T(8,128)}) custom-call(s32[1]{0:T(128)} %bitcast.pos_ref, bf16[2048,1536]{1,0:T(8,128)(2,1)} %get-tuple-element.51.h2_ref, ...), custom_call_target="tpu_custom_call" | custom-call | flops 32212254720 | bytes 62914560 | tf_op jit(solution)/shard_map/experts/pallas_call | solution.py:449
  247.2 14.7 %down_grad.1 = bf16[4,2,512,384]{3,2,1,0:T(8,128)(2,1)} custom-call(s32[1]{0:T(128)} %bitcast.pos_ref, bf16[2,2048,512]{2,1,0:T(8,128)(2,1)} %get-tuple-element.53.ag_ref, bf16[2048,1536]{1,0:T(8,128)(2,1)} %all-gather.5.cloned.1.call-done.dy_ref), custom_call_target="tpu_custom_call" | custom-call | flops 6442450944 | bytes 25165824 | tf_op jit(solution)/shard_map/down_grad/pallas_call | solution.py:487
  262.5 19.7 %up_grad.1 = bf16[2,1536,1024]{2,1,0:T(8,128)(2,1)} custom-call(s32[1]{0:T(128)} %bitcast.pos_ref, bf16[2048,1536]{1,0:T(8,128)(2,1)} %get-tuple-element.51.h2_ref, bf16[2,2048,1024]{2,1,0:T(8,128)(2,1)} %get-tuple-element.81.dgu_ref), custom_call_target="tpu_custom_call" | custom-call | flops 12884901888 | bytes 25165824 | tf_op jit(solution)/shard_map/up_grad/pallas_call | solution.py:512
  286.4 10.6 %collective-permute-done.26 = bf16[128,1536]{1,0:T(8,128)(2,1)S(1)} collective-permute-done((bf16[128,1536]{1,0:T(8,128)(2,1)S(1)}, bf16[128,1536]{1,0:T(8,128)(2,1)S(1)}, u32[]{:S(2)}, u32[]{:S(2)}) %collective-permute-start.26) | collective-permute-done | bytes 393248 | tf_op jit(solution)/shard_map/ppermute | solution.py:848
  304.1 12.7 %combine.1 = (bf16[4,256,1536]{2,1,0:T(8,128)(2,1)}, bf16[4,256,1536]{2,1,0:T(8,128)(2,1)}) custom-call(s32[1]{0:T(128)} %bitcast.pos_ref, bf16[2,2048,512]{2,1,0:T(8,128)(2,1)} %get-tuple-element.53.ag_ref, bf16[2,512,1536]{2,1,0:T(8,128)(2,1)} %down_ref.3), custom_call_target="tpu_custom_call" | custom-call | flops 6442450944 | bytes 12582912 | tf_op jit(solution)/shard_map/combine/pallas_call | solution.py:547
  321.4 8.0 %middle.1 = (f32[256,1536]{1,0:T(8,128)}, bf16[256,1536]{1,0:T(8,128)(2,1)}, bf16[8,192,256]{2,1,0:T(8,128)(2,1)}, f32[1536,128]{1,0:T(8,128)}, f32[8,1536]{1,0:T(8,128)}) custom-call(s32[1]{0:T(128)} %bitcast.pos_ref, bf16[4,256,1536]{2,1,0:T(8,128)(2,1)} %get-tuple-element.56.keep_ref, bf16[4,256,1536]{2,1,0:T(8,128)(2,1)} %collective-permute-done.23.got_ref, ...), custom_call_target="tpu_custom_call" | custom-call | flops 1207959552 | bytes 9437184 | tf_op jit(solution)/shard_map/middle/pallas_call | solution.py:604
  329.3 17.0 %all_to_all.44.da_ref = bf16[8,192,256]{2,1,0:T(8,128)(2,1)} all-to-all(bf16[8,192,256]{2,1,0:T(8,128)(2,1)} %get-tuple-element.61), channel_id=1, replica_groups=mesh['dp'=4,'expert'=8] {'expert'}, dimensions={0} | all-to-all | bytes 1572864 | tf_op jit(solution)/shard_map/all_to_all | solution.py:881
  346.4 28.9 %attn_bwd.1 = (f32[192,2048]{1,0:T(8,128)}, f32[64,2048]{1,0:T(8,128)}, f32[64,2048]{1,0:T(8,128)}) custom-call(s32[8]{0:T(128)} %and_select_fusion.first_ref, bf16[192,2048]{1,0:T(8,128)(2,1)} %get-tuple-element.46.q_ref, bf16[8,192,256]{2,1,0:T(8,128)(2,1)} %all_to_all.44.da_ref, f32[192,2048]{1,0:T(8,128)} %get-tuple-element.62.o_ref, ...), custom_call_target="tpu_custom_call" | custom-call | flops 8053063680 | bytes 4718592 | tf_op jit(solution)/shard_map/attn_bwd/pallas_call | solution.py:184
  375.2 10.6 %back.1 = (bf16[4,256,1536]{2,1,0:T(8,128)(2,1)}, bf16[4,256,1536]{2,1,0:T(8,128)(2,1)}, bf16[384,2048]{1,0:T(8,128)(2,1)}) custom-call(s32[1]{0:T(128)} %bitcast.pos_ref, f32[192,2048]{1,0:T(8,128)} %get-tuple-element.66.dq_ref, f32[64,2048]{1,0:T(8,128)} %get-tuple-element.67.dk_ref, f32[64,2048]{1,0:T(8,128)} %get-tuple-element.68.dv_ref, ...), custom_call_target="tpu_custom_call" | custom-call | flops 2415919104 | bytes 12582912 | tf_op jit(solution)/shard_map/back/pallas_call | solution.py:665
  397.1 6.6 %all-to-all-done.5 = bf16[8,256,192]{1,2,0:T(8,128)(2,1)S(1)} async-done(((bf16[8,256,192]{1,2,0:T(8,128)(2,1)}), bf16[8,256,192]{1,2,0:T(8,128)(2,1)S(1)}, u32[]{:S(2)}, u32[]{:S(2)}) %all-to-all-start.5) | async-done | bytes 786464 | tf_op jit(solution)/shard_map/all_to_all | solution.py:881
  405.0 9.1 %out_grad.1 = f32[192,1536]{1,0:T(8,128)} custom-call(s32[1]{0:T(128)} %bitcast.pos_ref, bf16[192,2048]{1,0:T(8,128)(2,1)} %get-tuple-element.49.refs_0_, bf16[192,2048]{1,0:T(8,128)(2,1)} %copy-done.16, bf16[192,2048]{1,0:T(8,128)(2,1)} %copy-done.6, bf16[192,2048]{1,0:T(8,128)(2,1)} %collective-permute-done.11.refs_3_, bf16[192,2048]{1,0:T(8,128)(2,1)} %copy-done.5, ...), custom_call_target="tpu_custom_call" | custom-call | flops 1207959552 | bytes 12582912 | tf_op jit(solution)/shard_map/out_grad/pallas_call | solution.py:798
  423.0 11.4 %pack.1 = bf16[1536,384]{1,0:T(8,128)(2,1)} custom-call(s32[1]{0:T(128)} %bitcast.pos_ref, bf16[384,2048]{1,0:T(8,128)(2,1)} %get-tuple-element.73.packed_ref, bf16[8,256,1536]{2,1,0:T(8,128)(2,1)} %bitcast.100, f32[1,1536]{1,0:T(1,128)} %reshape.200.refs_11_.gain_ref, f32[1536,128]{1,0:T(8,128)} %get-tuple-element.74.router_ref, ...), custom_call_target="tpu_custom_call" | custom-call | flops 2415919104 | bytes 12582912 | tf_op jit(solution)/shard_map/pack/pallas_call | solution.py:721
  438.2 8.3 %all-to-all-done.6 = bf16[4,48,1536]{2,1,0:T(8,128)(2,1)} async-done(((bf16[4,48,1536]{2,1,0:T(8,128)(2,1)}), bf16[4,48,1536]{2,1,0:T(8,128)(2,1)}, u32[]{:S(2)}, u32[]{:S(2)}) %all-to-all-start.6) | async-done | bytes 589856 | tf_op jit(solution)/shard_map/all_to_all | solution.py:881
  458.8 24.0 %collective-permute-done.22 = bf16[256,1536]{1,0:T(8,128)(2,1)S(1)} collective-permute-done((bf16[256,1536]{1,0:T(8,128)(2,1)S(1)}, bf16[256,1536]{1,0:T(8,128)(2,1)S(1)}, u32[]{:S(2)}, u32[]{:S(2)}) %collective-permute-start.22) | collective-permute-done | bytes 786464 | tf_op jit(solution)/shard_map/ppermute | solution.py:848
  492.9 6.4 %collective-permute-done.30.fx_ref = bf16[256,1536]{1,0:T(8,128)(2,1)S(1)} collective-permute-done((bf16[256,1536]{1,0:T(8,128)(2,1)S(1)}, bf16[256,1536]{1,0:T(8,128)(2,1)S(1)}, u32[]{:S(2)}, u32[]{:S(2)}) %collective-permute-start.30) | collective-permute-done | bytes 786464 | tf_op jit(solution)/shard_map/ppermute | solution.py:848
  513.0 5.7 %all-to-all-done.7 = f32[32,1,128]{2,1,0:T(1,128)S(1)} async-done(((f32[32,1,128]{2,1,0:T(1,128)}), f32[32,1,128]{2,1,0:T(1,128)S(1)}, u32[]{:S(2)}, u32[]{:S(2)}) %all-to-all-start.7) | async-done | bytes 16416 | tf_op jit(solution)/shard_map/all_to_all | solution.py:881
  (204 shorter events, 145.6 us)
Async XLA Ops:
  7.2 164.5 %all-gather.3.cloned.1.call-start = ((), (), s32[]{:S(2)}) async-start(), calls=%async_computation.10 | async-start | bytes 4866048 | tf_op jit(solution)/shard_map/all_gather | solution.py:942
  7.9 194.5 %all-gather.5.cloned.1.call-start = ((), (), s32[]{:S(2)}) async-start(), calls=%async_computation.11 | async-start | bytes 7077888 | tf_op jit(solution)/shard_map/all_gather | solution.py:943
  21.3 65.0 %all-to-all-start = ((bf16[32,48,384]{2,1,0:T(8,128)(2,1)}), bf16[32,48,384]{2,1,0:T(8,128)(2,1)S(1)}, u32[]{:S(2)}, u32[]{:S(2)}) async-start(bf16[32,48,384]{2,1,0:T(8,128)(2,1)} %bitcast.6), calls=%async_computation | async-start | bytes 2359296 | tf_op jit(solution)/shard_map/all_to_all | solution.py:881
  27.6 459.8 %reduce-scatter.5.cloned.1.call-start = ((), (), s32[]{:S(2)}) async-start(), calls=%async_computation.13 | async-start | bytes 3932160 | tf_op jit(solution)/shard_map/reduce_scatter | solution.py:971
  27.6 34.3 %collective-permute-start.3 = (bf16[256,1536]{1,0:T(8,128)(2,1)S(1)}, bf16[256,1536]{1,0:T(8,128)(2,1)S(1)}, u32[]{:S(2)}, u32[]{:S(2)}) collective-permute-start(bf16[256,1536]{1,0:T(8,128)(2,1)S(1)} %copy-done.4), channel_id=1, source_target_pairs={{0,4},{1,5},{2,6},{3,7},{4,0},{5,1},{6,2},{7,3},{8,12},{9,13},{10,... | collective-permute-start | bytes 2359304 | tf_op jit(solution)/shard_map/ppermute | solution.py:848
  29.5 34.7 %collective-permute-start.1 = (bf16[256,1536]{1,0:T(8,128)(2,1)S(1)}, bf16[256,1536]{1,0:T(8,128)(2,1)S(1)}, u32[]{:S(2)}, u32[]{:S(2)}) collective-permute-start(bf16[256,1536]{1,0:T(8,128)(2,1)S(1)} %copy-done.4), channel_id=1, source_target_pairs={{0,2},{1,3},{2,0},{3,1},{4,6},{5,7},{6,4},{7,5},{8,10},{9,11},{10,... | collective-permute-start | bytes 2359304 | tf_op jit(solution)/shard_map/ppermute | solution.py:848
  30.9 53.3 %collective-permute-start = (bf16[256,1536]{1,0:T(8,128)(2,1)S(1)}, bf16[256,1536]{1,0:T(8,128)(2,1)}, u32[]{:S(2)}, u32[]{:S(2)}) collective-permute-start(bf16[256,1536]{1,0:T(8,128)(2,1)S(1)} %copy-done.4), channel_id=1, source_target_pairs={{0,1},{1,0},{2,3},{3,2},{4,5},{5,4},{6,7},{7,6},{8,9},{9,8},{10,11... | collective-permute-start | bytes 2359304 | tf_op jit(solution)/shard_map/ppermute | solution.py:848
  119.9 35.0 %collective-permute-start.12 = (bf16[192,2048]{1,0:T(8,128)(2,1)}, bf16[192,2048]{1,0:T(8,128)(2,1)S(1)}, u32[]{:S(2)}, u32[]{:S(2)}) collective-permute-start(bf16[192,2048]{1,0:T(8,128)(2,1)} %get-tuple-element.49.refs_0_), channel_id=1, source_target_pairs={{0,4},{1,5},{2,6},{3,7},{4,0},{5,1},{6,2},{7,3},{8,12},{9,13},{10,... | collective-permute-start | bytes 2359304 | tf_op jit(solution)/shard_map/ppermute | solution.py:848
  121.6 34.9 %collective-permute-start.10 = (bf16[192,2048]{1,0:T(8,128)(2,1)}, bf16[192,2048]{1,0:T(8,128)(2,1)S(1)}, u32[]{:S(2)}, u32[]{:S(2)}) collective-permute-start(bf16[192,2048]{1,0:T(8,128)(2,1)} %get-tuple-element.49.refs_0_), channel_id=1, source_target_pairs={{0,2},{1,3},{2,0},{3,1},{4,6},{5,7},{6,4},{7,5},{8,10},{9,11},{10,... | collective-permute-start | bytes 2359304 | tf_op jit(solution)/shard_map/ppermute | solution.py:848
  128.2 50.2 %collective-permute-start.9 = (bf16[192,2048]{1,0:T(8,128)(2,1)S(1)}, bf16[192,2048]{1,0:T(8,128)(2,1)S(1)}, u32[]{:S(2)}, u32[]{:S(2)}) collective-permute-start(bf16[192,2048]{1,0:T(8,128)(2,1)S(1)} %copy-done.15), channel_id=1, source_target_pairs={{0,1},{1,0},{2,3},{3,2},{4,5},{5,4},{6,7},{7,6},{8,9},{9,8},{10,11... | collective-permute-start | bytes 2359304 | tf_op jit(solution)/shard_map/ppermute | solution.py:848
  157.1 21.3 %collective-permute-start.13 = (bf16[192,2048]{1,0:T(8,128)(2,1)S(1)}, bf16[192,2048]{1,0:T(8,128)(2,1)}, u32[]{:S(2)}, u32[]{:S(2)}) collective-permute-start(bf16[192,2048]{1,0:T(8,128)(2,1)S(1)} %collective-permute-done.12.refs_4_), channel_id=1, source_target_pairs={{0,1},{1,0},{2,3},{3,2},{4,5},{5,4},{6,7},{7,6},{8,9},{9,8},{10,11... | collective-permute-start | bytes 2359304 | tf_op jit(solution)/shard_map/ppermute | solution.py:848
  157.1 21.3 %collective-permute-start.11 = (bf16[192,2048]{1,0:T(8,128)(2,1)S(1)}, bf16[192,2048]{1,0:T(8,128)(2,1)}, u32[]{:S(2)}, u32[]{:S(2)}) collective-permute-start(bf16[192,2048]{1,0:T(8,128)(2,1)S(1)} %collective-permute-done.10.refs_2_), channel_id=1, source_target_pairs={{0,1},{1,0},{2,3},{3,2},{4,5},{5,4},{6,7},{7,6},{8,9},{9,8},{10,11... | collective-permute-start | bytes 2359304 | tf_op jit(solution)/shard_map/ppermute | solution.py:848
  261.9 257.4 %reduce-scatter.3.cloned.1.call-start = ((), (), s32[]{:S(2)}) async-start(), calls=%async_computation.12 | async-start | bytes 7864320 | tf_op jit(solution)/shard_map/reduce_scatter | solution.py:975
  298.6 21.5 %collective-permute-start.25 = (bf16[256,1536]{1,0:T(8,128)(2,1)S(1)}, bf16[256,1536]{1,0:T(8,128)(2,1)S(1)}, u32[]{:S(2)}, u32[]{:S(2)}) collective-permute-start(bf16[256,1536]{1,0:T(8,128)(2,1)S(1)} %pad_maximum_fusion.2), channel_id=1, source_target_pairs={{0,2},{1,3},{2,0},{3,1},{4,6},{5,7},{6,4},{7,5},{8,10},{9,11},{10,... | collective-permute-start | bytes 2359304 | tf_op jit(solution)/shard_map/ppermute | solution.py:848
  316.8 73.9 %collective-permute-start.18 = (bf16[4,256,1536]{2,1,0:T(8,128)(2,1)}, bf16[4,256,1536]{2,1,0:T(8,128)(2,1)}, u32[]{:S(2)}, u32[]{:S(2)}) collective-permute-start(bf16[4,256,1536]{2,1,0:T(8,128)(2,1)} %get-tuple-element.55), channel_id=1, source_target_pairs={{0,1},{1,0},{2,3},{3,2},{4,5},{5,4},{6,7},{7,6},{8,9},{9,8},{10,11... | collective-permute-start | bytes 9437192 | tf_op jit(solution)/shard_map/ppermute | solution.py:848
  385.8 48.6 %collective-permute-start.28 = (bf16[4,256,1536]{2,1,0:T(8,128)(2,1)}, bf16[4,256,1536]{2,1,0:T(8,128)(2,1)}, u32[]{:S(2)}, u32[]{:S(2)}) collective-permute-start(bf16[4,256,1536]{2,1,0:T(8,128)(2,1)} %get-tuple-element.70), channel_id=1, source_target_pairs={{0,1},{1,0},{2,3},{3,2},{4,5},{5,4},{6,7},{7,6},{8,9},{9,8},{10,11... | collective-permute-start | bytes 9437192 | tf_op jit(solution)/shard_map/ppermute | solution.py:848
  393.7 26.8 %collective-permute-start.21 = (bf16[128,1536]{1,0:T(8,128)(2,1)S(1)}, bf16[128,1536]{1,0:T(8,128)(2,1)S(1)}, u32[]{:S(2)}, u32[]{:S(2)}) collective-permute-start(bf16[128,1536]{1,0:T(8,128)(2,1)S(1)} %get-tuple-element.138), channel_id=1, source_target_pairs={{0,2},{1,3},{2,0},{3,1},{4,6},{5,7},{6,4},{7,5},{8,10},{9,11},{10,... | collective-permute-start | bytes 1179656 | tf_op jit(solution)/shard_map/ppermute | solution.py:848
  395.6 24.9 %collective-permute-start.19 = (bf16[128,1536]{1,0:T(8,128)(2,1)S(1)}, bf16[128,1536]{1,0:T(8,128)(2,1)S(1)}, u32[]{:S(2)}, u32[]{:S(2)}) collective-permute-start(bf16[128,1536]{1,0:T(8,128)(2,1)S(1)} %get-tuple-element.139), channel_id=1, source_target_pairs={{0,4},{1,5},{2,6},{3,7},{4,0},{5,1},{6,2},{7,3},{8,12},{9,13},{10,... | collective-permute-start | bytes 1179656 | tf_op jit(solution)/shard_map/ppermute | solution.py:848
  416.3 30.2 %all-to-all-start.6 = ((bf16[4,48,1536]{2,1,0:T(8,128)(2,1)}), bf16[4,48,1536]{2,1,0:T(8,128)(2,1)}, u32[]{:S(2)}, u32[]{:S(2)}) async-start(bf16[4,48,1536]{2,1,0:T(8,128)(2,1)} %bitcast.40), calls=%async_computation.6 | async-start | bytes 1179648 | tf_op jit(solution)/shard_map/all_to_all | solution.py:881
  446.5 43.3 %all-to-all-start.4 = ((bf16[32,48,384]{2,1,0:T(8,128)(2,1)}), bf16[32,48,384]{2,1,0:T(8,128)(2,1)}, u32[]{:S(2)}, u32[]{:S(2)}) async-start(bf16[32,48,384]{2,1,0:T(8,128)(2,1)} %bitcast.101), calls=%async_computation.4 | async-start | bytes 2359296 | tf_op jit(solution)/shard_map/all_to_all | solution.py:881
  451.5 31.3 %collective-permute-start.22 = (bf16[256,1536]{1,0:T(8,128)(2,1)S(1)}, bf16[256,1536]{1,0:T(8,128)(2,1)S(1)}, u32[]{:S(2)}, u32[]{:S(2)}) collective-permute-start(bf16[256,1536]{1,0:T(8,128)(2,1)S(1)} %pad_maximum_fusion.1), channel_id=1, source_target_pairs={{0,4},{1,5},{2,6},{3,7},{4,0},{5,1},{6,2},{7,3},{8,12},{9,13},{10,... | collective-permute-start | bytes 2359304 | tf_op jit(solution)/shard_map/ppermute | solution.py:848
  454.4 28.4 %collective-permute-start.20 = (bf16[256,1536]{1,0:T(8,128)(2,1)S(1)}, bf16[256,1536]{1,0:T(8,128)(2,1)S(1)}, u32[]{:S(2)}, u32[]{:S(2)}) collective-permute-start(bf16[256,1536]{1,0:T(8,128)(2,1)S(1)} %pad_maximum_fusion), channel_id=1, source_target_pairs={{0,2},{1,3},{2,0},{3,1},{4,6},{5,7},{6,4},{7,5},{8,10},{9,11},{10,... | collective-permute-start | bytes 2359304 | tf_op jit(solution)/shard_map/ppermute | solution.py:848
  457.6 41.8 %collective-permute-start.30 = (bf16[256,1536]{1,0:T(8,128)(2,1)S(1)}, bf16[256,1536]{1,0:T(8,128)(2,1)S(1)}, u32[]{:S(2)}, u32[]{:S(2)}) collective-permute-start(bf16[256,1536]{1,0:T(8,128)(2,1)S(1)} %pad_maximum_fusion.4), channel_id=1, source_target_pairs={{0,2},{1,3},{2,0},{3,1},{4,6},{5,7},{6,4},{7,5},{8,10},{9,11},{10,... | collective-permute-start | bytes 2359304 | tf_op jit(solution)/shard_map/ppermute | solution.py:848
  458.3 41.1 %collective-permute-start.32 = (bf16[256,1536]{1,0:T(8,128)(2,1)S(1)}, bf16[256,1536]{1,0:T(8,128)(2,1)S(1)}, u32[]{:S(2)}, u32[]{:S(2)}) collective-permute-start(bf16[256,1536]{1,0:T(8,128)(2,1)S(1)} %pad_maximum_fusion.5), channel_id=1, source_target_pairs={{0,4},{1,5},{2,6},{3,7},{4,0},{5,1},{6,2},{7,3},{8,12},{9,13},{10,... | collective-permute-start | bytes 2359304 | tf_op jit(solution)/shard_map/ppermute | solution.py:848
  (45 other events, 600.5 us)
Sparse Core Ops, SparseCore 0:
  10.9 82.4 all-gather.2
  95.3 59.3 all-gather.4
  262.0 59.4 reduce-scatter.4
  323.7 118.6 reduce-scatter.2
where the time goes:
time: 534 us; the launch traced here: 530 us
  Pallas kernels  222 us (42%)
  waiting for transfers between devices  139 us (26%)
  starting transfers between devices  55.1 us (10%)
  local copies, waits for them, and re-layouts  46 us (9%)
  other arithmetic  35.3 us (7%)
  blocking collectives  17 us (3%)
  between operations  14.7 us (3%)
    ppermute x33, waiting for transfers between devices, swap(): return lax.ppermute(values, 'expert', [(i, i ^ bit) for i in range(count)])  115 us
    pallas_call x1, Pallas kernels, expert_main(): call(functools.partial(expert_kernel, half), 'experts', (steps,), [spec((...  44.8 us
    all_to_all x7, starting transfers between devices, exchange(): return lax.all_to_all(blocks, axes, split_axis=0, concat_axis=0, tiled=True)  30.8 us
    pallas_call x1, Pallas kernels, attn_backward(): pl.pallas_call(attn_bwd_kernel, grid_spec=pltpu.PrefetchScalarGridSpec(nu...  28.9 us
    ppermute x33, starting transfers between devices, swap(): return lax.ppermute(values, 'expert', [(i, i ^ bit) for i in range(count)])  24.2 us
    pallas_call x1, Pallas kernels, attn_forward(): pl.pallas_call(attn_fwd_kernel, grid_spec=pltpu.PrefetchScalarGridSpec(nu...  23.2 us
    pallas_call x1, Pallas kernels, mix_forward(): call(functools.partial(mix_kernel, count), 'mix', (seq // BLK,), [spec((a...  23.1 us
    all_to_all x7, waiting for transfers between devices, exchange(): return lax.all_to_all(blocks, axes, split_axis=0, concat_axis=0, tiled=True)  22.9 us
  transfers between devices with their start and end apart: 44, of which 16 were waited for; matrix products, arithmetic and copies ran while one was open for 14% of the time, Pallas kernels for 31%

commit v1 on v0

--- a/solution.py
+++ b/solution.py
@@ -28,6 +28,13 @@
 BF = jnp.bfloat16
 F32 = jnp.float32
 BOTH = ("dp", "expert")
+
+
+def cost(micros):
+    return pl.CostEstimate(flops=micros * 10**9, bytes_accessed=10**4, transcendentals=0)
+
+
+LONG, SHORT = cost(50), cost(0)
 
 
 def dot(a, b, ca, cb):
@@ -169,9 +176,7 @@
             jax.ShapeDtypeStruct((rows, seq), F32),
             jax.ShapeDtypeStruct((8, seq), F32),
         ],
-        cost_estimate=pl.CostEstimate(
-            flops=4 * rows * seq * seq, bytes_accessed=8 * rows * seq, transcendentals=GROUP * seq * seq
-        ),
+        cost_estimate=LONG,
         name="attn_fwd",
     )(first, q_t, k, v_t, start)
 
@@ -211,9 +216,7 @@
             jax.ShapeDtypeStruct((HEAD_DIM, seq), F32),
             jax.ShapeDtypeStruct((HEAD_DIM, seq), F32),
         ],
-        cost_estimate=pl.CostEstimate(
-            flops=10 * rows * seq * seq, bytes_accessed=12 * rows * seq, transcendentals=GROUP * seq * seq
-        ),
+        cost_estimate=cost(20),
         name="attn_bwd",
     )(first, q_t, da, o_t, lse, k, k_t, v, start)
 
@@ -234,7 +237,7 @@
     )
 
 
-def call(kernel, name, grid, in_specs, out_specs, out_shape, flops, moved, scratch=()):
+def call(kernel, name, grid, in_specs, out_specs, out_shape, estimate, scratch=()):
     return pl.pallas_call(
         kernel,
         grid_spec=pltpu.PrefetchScalarGridSpec(
@@ -245,7 +248,7 @@
             scratch_shapes=list(scratch),
         ),
         out_shape=out_shape,
-        cost_estimate=pl.CostEstimate(flops=flops, bytes_accessed=moved, transcendentals=0),
+        cost_estimate=estimate,
         name=name,
     )
 
@@ -324,9 +327,35 @@
             shape((seq, HEAD_DIM), BF),
             shape((seq, HEAD_DIM), BF),
         ],
-        2 * seq * D * PACK,
-        2 * seq * D,
+        cost(400),
     )(pos, *pieces, weights, gain, cosine, sine)
+
+
+def send_weights_kernel(groups, members, pos_ref, q_ref, kv_ref, rest_ref, out_ref):
+    query, pair, rest = q_ref[...], kv_ref[...], rest_ref[...]
+    for j in range(members):
+        block = jnp.concatenate(
+            [query[:, j * Q_COLS : (j + 1) * Q_COLS]]
+            + [pair[:, n * HEAD_DIM : (n + 1) * HEAD_DIM] for n in (j, members + j)]
+            + [rest],
+            axis=1,
+        )
+        for i in range(groups):
+            out_ref[i * members + j] = block
+
+
+def send_weights(pos, w_query, w_key_value, rest, groups, members):
+    rows = w_query.shape[0]
+    full = lambda a: resident(a.shape)
+    return call(
+        functools.partial(send_weights_kernel, groups, members),
+        "send_weights",
+        (1,),
+        [full(a) for a in (w_query, w_key_value, rest)],
+        resident((groups * members, rows, PACK)),
+        shape((groups * members, rows, PACK), BF),
+        SHORT,
+    )(pos, w_query, w_key_value, rest)
 
 
 def mix_kernel(count, pos_ref, *refs):
@@ -348,7 +377,7 @@
     h2 = (norm_of(y1) * gain_ref[...]).astype(BF)
     logits = dot(h2, route_ref[...], 1, 0)
     lane = lax.broadcasted_iota(jnp.int32, logits.shape, 1) - ROUTE
-    ids = ids_ref[...]
+    ids = ids_ref[0].T
     chosen = lane == ids[:, 0:1]
     for k in range(1, TOP):
         chosen = chosen | (lane == ids[:, k : k + 1])
@@ -367,7 +396,7 @@
 
 def mix_forward(pos, pieces, x_rel, w_full, gain, weights, ids):
     count = len(pieces) - 2
-    seq = ids.shape[0]
+    seq = ids.shape[0] * BLK
     row = lambda s, pos: (s, 0)
     return call(
         functools.partial(mix_kernel, count),
@@ -379,7 +408,7 @@
             resident(w_full.shape),
             resident(gain.shape),
             pl.BlockSpec((D, 128), lambda s, pos: (0, 2), pipeline_mode=pl.Buffered(1)),
-            spec((BLK, TOP), row),
+            spec((1, TOP, BLK), lambda s, pos: (s ^ pos[0], 0, 0)),
         ],
         [
             spec((BLK, D), row),
@@ -395,8 +424,7 @@
             shape((BLK, D), BF),
             shape((BLK, 128), F32),
         ],
-        2 * seq * D * D,
-        10 * seq * D,
+        LONG,
         [pltpu.VMEM((HEADS * HEAD_DIM, BLK), BF)],
     )(pos, *pieces, x_rel, w_full, gain, weights, ids)
 
@@ -471,8 +499,7 @@
             shape((EXP_DEV, seq, 2 * FF), BF),
             shape((steps, 8, BLK), F32),
         ],
-        10 * EXP_DEV * seq * D * FF,
-        20 * seq * D,
+        LONG,
     )(pos, h2, dy_all, gates, w_gate_up, w_down)
 
 
@@ -494,8 +521,7 @@
         ],
         spec((1, 1, FF, wide), lambda e, s, pos: (s, e, 0, 0)),
         shape((D // wide, EXP_DEV, FF, wide), BF),
-        2 * EXP_DEV * seq * D * FF,
-        8 * seq * D,
+        SHORT,
     )(pos, ag, dy_all)
     if wide == cols:
         return out
@@ -519,8 +545,7 @@
         ],
         spec((1, rows, 2 * FF), lambda e, s, pos: (e, s, 0)),
         shape((EXP_DEV, D, 2 * FF), BF),
-        4 * EXP_DEV * seq * D * FF,
-        8 * seq * D,
+        SHORT,
     )(pos, h2, dgu)
     return out
 
@@ -557,8 +582,7 @@
             spec((1, BLK, D), lambda s, pos: (keep_index(s, half), 0, 0)),
         ],
         [shape((half, BLK, D), BF), shape((half, BLK, D), BF)],
-        2 * EXP_DEV * seq * D * FF,
-        4 * seq * D,
+        SHORT,
     )(pos, ag, w_down)
 
 
@@ -571,7 +595,7 @@
 
 
 def middle_kernel(
-    pos_ref, keep_ref, got_ref, fx_ref, fy_ref, y1_ref, h2_ref, gates_ref, dg_ref, dy_ref,
+    members, groups, wide, pos_ref, keep_ref, got_ref, fx_ref, fy_ref, fd_ref, y1_ref, h2_ref, gates_ref, dg_ref, dy_ref,
     route_ref, gain_ref, w_ref, dy1_ref, db_ref, da_ref, router_ref, gain_grad_ref,
 ):
     dh2 = (
@@ -579,6 +603,7 @@
         + got_ref[0].astype(F32)
         + fx_ref[...].astype(F32)
         + fy_ref[...].astype(F32)
+        + fd_ref[...].astype(F32)
     )
     gates, gate_grads = gates_ref[...], dg_ref[...]
     mean = jnp.sum(gates * gate_grads, axis=1, keepdims=True)
@@ -592,21 +617,30 @@
     db = (RESIDUAL * dy1).astype(BF)
     db_ref[...] = db
     da = dot(w_ref[...], db, 1, 1).astype(BF)
-    for j in range(da_ref.shape[0]):
-        da_ref[j] = da[j * Q_COLS : (j + 1) * Q_COLS]
-
-
-def middle(pos, keep, got, fx, fy, y1, h2, gates, dg, dy, weights, gain, w_full):
+    for j in range(members):
+        da_ref[j, :Q_COLS] = da[j * Q_COLS : (j + 1) * Q_COLS]
+    if wide:
+        cols = Q_COLS // groups
+        db_t = (RESIDUAL * dy1).T.astype(BF)
+        for j in range(members):
+            for i in range(groups):
+                at, to = (i * members + j) * cols, Q_COLS + i * cols
+                da_ref[j, to : to + cols] = db_t[at : at + cols]
+
+
+def middle(groups, pos, keep, got, sums, y1, h2, gates, dg, dy, weights, gain, w_full):
     rows = y1.shape[0]
     full = lambda a: resident(a.shape)
     first = pl.BlockSpec((1, rows, D), lambda s, pos: (0, 0, 0), pipeline_mode=pl.Buffered(1))
     members = HEADS * HEAD_DIM // Q_COLS
-    return call(
-        middle_kernel,
+    wide = Q_COLS // groups % 16 == 0
+    both = 2 * Q_COLS if wide else Q_COLS
+    dy1, db, sent, router, gain_grad = call(
+        functools.partial(middle_kernel, members, groups, wide),
         "middle",
         (1,),
         [first, first]
-        + [full(a) for a in (fx, fy, y1, h2, gates, dg, dy)]
+        + [full(a) for a in (*sums, y1, h2, gates, dg, dy)]
         + [
             pl.BlockSpec((D, 128), lambda s, pos: (0, 2), pipeline_mode=pl.Buffered(1)),
             full(gain),
@@ -615,20 +649,24 @@
         [
             resident((rows, D)),
             resident((rows, D)),
-            resident((members, Q_COLS, rows)),
+            resident((members, both, rows)),
             resident((D, 128)),
             resident((8, D)),
         ],
         [
             shape((rows, D), F32),
             shape((rows, D), BF),
-            shape((members, Q_COLS, rows), BF),
+            shape((members, both, rows), BF),
             shape((D, 128), F32),
             shape((8, D), F32),
         ],
-        2 * rows * D * D,
-        4 * D * D,
-    )(pos, keep, got, fx, fy, y1, h2, gates, dg, dy, weights, gain, w_full)
+        cost(100),
+    )(pos, keep, got, *sums, y1, h2, gates, dg, dy, weights, gain, w_full)
+    if not wide:
+        cols = Q_COLS // groups
+        db_t = jnp.moveaxis(db.T.reshape(groups, members, cols, rows), 1, 0)
+        sent = jnp.concatenate([sent, db_t.reshape(members, Q_COLS, rows)], axis=1)
+    return dy1, sent, router, gain_grad
 
 
 def back_kernel(
@@ -684,8 +722,7 @@
             shape((half, BLK, D), BF),
             shape((PACK, seq), BF),
         ],
-        2 * seq * D * PACK,
-        4 * seq * D,
+        cost(10),
     )(pos, dq_t, dk_t, dv_t, cosine, sine, weights)
 
 
@@ -694,7 +731,7 @@
     return high, values - high
 
 
-def pack_kernel(pos_ref, packed_ref, x_ref, gain_ref, router_ref, moe_ref, out_ref, acc):
+def pack_kernel(pos_ref, packed_ref, x_ref, gain_ref, w_ref, router_ref, moe_ref, out_ref, acc):
     step = pl.program_id(0)
 
     @pl.when(step == 0)
@@ -706,17 +743,24 @@
 
     @pl.when(step == pl.num_programs(0) - 1)
     def _():
-        out_ref[:, :256] = acc[:256].T.astype(BF)
+        main, rest = acc[:256].T, acc[256:].T
+        w_main, w_rest = w_ref[:, :256].astype(F32), w_ref[:, 256:].astype(F32)
         lane = lax.broadcasted_iota(jnp.int32, (D, 128), 1)
+        gain_attn = (
+            jnp.sum(main * w_main, axis=1, keepdims=True)
+            + jnp.sum(rest * w_rest, axis=1, keepdims=True)
+        ) / w_rest[:, ROUTE + 16 : ROUTE + 17]
         high, low = low_pair(router_ref[...])
-        gain_high, gain_low = low_pair(moe_ref[...].T)
-        rest = acc[256:].T + high + pltpu.roll(low, 16, 1)
-        rest = jnp.where(lane == ROUTE + 32, gain_high[:, :1], rest)
-        rest = jnp.where(lane == ROUTE + 33, gain_low[:, :1], rest)
+        moe_high, moe_low = low_pair(moe_ref[...].T)
+        attn_high, attn_low = low_pair(gain_attn)
+        rest = rest + high + pltpu.roll(low, 16, 1)
+        for at, column in enumerate((moe_high[:, :1], moe_low[:, :1], attn_high, attn_low)):
+            rest = jnp.where(lane == ROUTE + 32 + at, column, rest)
+        out_ref[:, :256] = main.astype(BF)
         out_ref[:, 256:] = rest.astype(BF)
 
 
-def pack(pos, packed, x_rel, gain, router, moe):
+def pack(pos, packed, x_rel, gain, weights, router, moe):
     seq = packed.shape[1]
     return call(
         pack_kernel,
@@ -726,32 +770,32 @@
             spec((PACK, BLK), lambda s, pos: (0, s)),
             spec((1, BLK, D), lambda s, pos: (s ^ pos[0], 0, 0)),
             resident(gain.shape),
+            resident(weights.shape),
             resident(router.shape),
             resident(moe.shape),
         ],
         resident((D, PACK)),
         shape((D, PACK), BF),
-        2 * seq * D * PACK,
-        4 * seq * D,
+        SHORT,
         [pltpu.VMEM((PACK, D), F32)],
-    )(pos, packed, x_rel, gain, router, moe)
+    )(pos, packed, x_rel, gain, weights, router, moe)
 
 
 def last_kernel(
-    pos_ref, keep_ref, got_ref, fx_ref, fy_ref, x_ref, gain_ref, dy1_ref, out_ref, gain_grad_ref
+    pos_ref, keep_ref, got_ref, fx_ref, fy_ref, fd_ref, x_ref, gain_ref, dy1_ref, out_ref
 ):
     dh1 = (
         keep_ref[0].astype(F32)
         + got_ref[0].astype(F32)
         + fx_ref[...].astype(F32)
         + fy_ref[...].astype(F32)
-    )
-    pulled, gain_grad = norm_pull(x_ref[...].astype(F32), gain_ref[...], dh1)
+        + fd_ref[...].astype(F32)
+    )
+    pulled, _ = norm_pull(x_ref[...].astype(F32), gain_ref[...], dh1)
     out_ref[...] = (dy1_ref[...] + pulled).astype(BF)
-    gain_grad_ref[...] = jnp.broadcast_to(gain_grad, gain_grad_ref.shape)
-
-
-def last(pos, keep, got, fx, fy, x, gain, dy1):
+
+
+def last(pos, keep, got, sums, x, gain, dy1):
     rows = x.shape[0]
     full = lambda a: resident(a.shape)
     first = pl.BlockSpec((1, rows, D), lambda s, pos: (0, 0, 0), pipeline_mode=pl.Buffered(1))
@@ -759,12 +803,11 @@
         last_kernel,
         "last",
         (1,),
-        [first, first] + [full(a) for a in (fx, fy, x, gain, dy1)],
-        [resident((rows, D)), resident((8, D))],
-        [shape((rows, D), BF), shape((8, D), F32)],
-        20 * rows * D,
-        14 * rows * D,
-    )(pos, keep, got, fx, fy, x, gain, dy1)
+        [first, first] + [full(a) for a in (*sums, x, gain, dy1)],
+        resident((rows, D)),
+        shape((rows, D), BF),
+        cost(50),
+    )(pos, keep, got, *sums, x, gain, dy1)
 
 
 def out_grad_kernel(count, pos_ref, *refs):
@@ -781,7 +824,7 @@
             at = count - 2 + 2 * (r - count + 2)
             heads[pl.ds(pl.multiple_of(base, half), half), :] = pieces[at][...]
             heads[pl.ds(pl.multiple_of(base + half, half), half), :] = pieces[at + 1][...]
-    term = dot(db_ref[...], heads[...], 0, 1)
+    term = dot(db_ref[0], heads[...], 1, 1)
 
     @pl.when(step == 0)
     def _():
@@ -792,21 +835,20 @@
         out_ref[...] += term
 
 
-def out_grad(pos, pieces, db_cols):
+def out_grad(pos, pieces, came):
     count = len(pieces) - 2
-    seq, cols = db_cols.shape
+    seq, cols = came.shape[0] * BLK, Q_COLS
     return call(
         functools.partial(out_grad_kernel, count),
         "out_grad",
         (seq // BLK,),
         [spec((a.shape[0], BLK), lambda s, pos: (0, s)) for a in pieces]
-        + [spec((BLK, cols), lambda s, pos: (s, 0))],
+        + [spec((1, cols, BLK), lambda s, pos: (s, 1, 0))],
         resident((cols, HEADS * HEAD_DIM)),
         shape((cols, HEADS * HEAD_DIM), F32),
-        2 * seq * D * cols,
-        4 * seq * D,
+        SHORT,
         [pltpu.VMEM((HEADS * HEAD_DIM, BLK), BF)],
-    )(pos, *pieces, db_cols).astype(BF)
+    )(pos, *pieces, came).astype(BF)
 
 
 def unpack_kernel(groups, members, pos_ref, came_ref, query_ref, pair_ref, rest_ref):
@@ -838,8 +880,7 @@
             shape((rows, 2 * KV_HEADS * HEAD_DIM), F32),
             shape((rows, 128), F32),
         ],
-        devices * rows * PACK,
-        4 * devices * rows * PACK,
+        SHORT,
     )(pos, came)
 
 
@@ -848,33 +889,42 @@
     return lax.ppermute(values, "expert", [(i, i ^ bit) for i in range(count)])
 
 
-def gather_pieces(own):
+def gather_pieces(own, before_last):
     half = own.shape[0] // 2
     x, y = swap(own, 2), swap(own, 4)
     core = swap(own, 1)
-    far_a, far_b = swap(x[:half], 4), swap(y[half:], 2)
+    far_a, far_b = tie((swap(x[:half], 4), swap(y[half:], 2)), before_last)
     return [
         own, core, x, swap(x, 1), y, swap(y, 1),
         far_a, far_b, swap(far_a, 1), swap(far_b, 1),
     ]
 
 
-def scatter_sum(give, keep):
-    half = keep.shape[1] // 2
-    got = swap(give, 1)
-
-    def pair(which, low, high):
-        return keep[which, low:high].astype(F32) + got[which, low:high].astype(F32)
-
-    far_a = swap(pair(3, 0, half).astype(BF), 2)
-    far_b = swap(pair(3, half, 2 * half).astype(BF), 4)
-    via_y = jnp.concatenate(
-        [pair(2, 0, half) + far_a.astype(F32), pair(2, half, 2 * half)], axis=0
-    ).astype(BF)
-    via_x = jnp.concatenate(
-        [pair(1, 0, half), pair(1, half, 2 * half) + far_b.astype(F32)], axis=0
-    ).astype(BF)
-    return got, swap(via_x, 2), swap(via_y, 4)
+def gather_direct(own):
+    near = [own, swap(own, 2), swap(own, 4), swap(own, 6)]
+    return [piece for value in near for piece in (value, swap(value, 1))]
+
+
+def tie(values, *after):
+    return lax.optimization_barrier((values, after))[0]
+
+
+def pair_sums(keep, got):
+    return [(keep[r].astype(F32) + got[r].astype(F32)).astype(BF) for r in (1, 2, 3)]
+
+
+def send_sums(sums):
+    return [swap(sums[0], 2), swap(sums[1], 4), swap(sums[2], 6)]
+
+
+def send_to_groups(blocks):
+    count = lax.axis_size("dp")
+    me = lax.axis_index("dp")
+    terms = [lax.dynamic_index_in_dim(blocks, me, 0, False)]
+    for k in range(1, count):
+        sent = lax.dynamic_index_in_dim(blocks, (me + k) % count, 0, False)
+        terms.append(lax.ppermute(sent, "dp", [(i, (i + k) % count) for i in range(count)]))
+    return terms
 
 
 def exchange(blocks, axes):
@@ -907,40 +957,21 @@
     out_cols = w_out.shape[1]
     kv_cols = KV_HEADS * HEAD_DIM
 
-    x_pieces = gather_pieces(tokens)
-
-    own = jnp.concatenate(
-        [
-            w_query.reshape(in_rows, members, Q_COLS),
-            w_key_value[:, :kv_cols].reshape(in_rows, members, HEAD_DIM),
-            w_key_value[:, kv_cols:].reshape(in_rows, members, HEAD_DIM),
-            jnp.broadcast_to(
-                jnp.concatenate(
-                    [
-                        w_router,
-                        norm_attn[:, None],
-                        norm_moe[:, None],
-                        jnp.zeros((in_rows, PACK - QKV - expert_total - 2), BF),
-                    ],
-                    axis=1,
-                )[:, None, :],
-                (in_rows, members, PACK - QKV),
-            ),
-        ],
-        axis=2,
-    )
-    own = jnp.moveaxis(own, 1, 0)
-    own = jnp.broadcast_to(own[None], (groups,) + own.shape).reshape(devices, in_rows, PACK)
+    x_pieces = gather_pieces(tokens, ())
+
+    rest = jnp.concatenate(
+        [
+            w_router,
+            norm_attn[:, None],
+            norm_moe[:, None],
+            jnp.zeros((in_rows, PACK - QKV - expert_total - 2), BF),
+        ],
+        axis=1,
+    )
+    own = send_weights(pos, w_query, w_key_value, rest, groups, members)
     weights = exchange(own, BOTH).reshape(D, PACK)
     gain_attn = weights[:, QKV + expert_total].astype(F32)[None]
     gain_moe = weights[:, QKV + expert_total + 1].astype(F32)[None]
-
-    ids_t = exchange(
-        jnp.broadcast_to(expert_ids.T[None], (members, TOP, tok_rows)), "expert"
-    )
-    ids = jnp.moveaxis(ids_t.reshape(members, TOP, tok_rows), 1, 2).reshape(seq, TOP)
-    w_full = lax.all_gather(w_out.T, BOTH, axis=0, tiled=True).T
-    dy_all = lax.all_gather(grad_out, "expert", axis=0, tiled=True)
 
     token_pos = jnp.arange(seq, dtype=jnp.int32)
     start = jnp.sum(
@@ -951,58 +982,58 @@
     angles = frequency[:, None] * token_pos.astype(F32)[None, :]
     cosine, sine = jnp.cos(angles), jnp.sin(angles)
 
-    q_t, k_t, v_t, k, v = qkv_forward(pos, x_pieces, weights, gain_attn, cosine, sine)
+    q_t, k_t, v_t, k, v = qkv_forward(
+        pos, x_pieces, tie(weights, start, first), gain_attn, cosine, sine
+    )
+    w_full = lax.all_gather(tie(w_out.T, q_t), BOTH, axis=0, tiled=True)
+    dy_all = lax.all_gather(tie(grad_out, q_t), "expert", axis=0, tiled=True)
+    w_full = w_full.T
     a_t, o_t, lse = attn_forward(first, q_t, k, v_t, start)
-    a_pieces = gather_pieces(a_t)
-    x_rel = jnp.concatenate(
-        [piece for piece in x_pieces], axis=0
-    ).reshape(members, tok_rows, D)
+    ids = jnp.concatenate(gather_direct(tie(expert_ids, q_t).T), axis=0)
+    ids = ids.reshape(members, TOP, tok_rows)
+    a_pieces = gather_pieces(a_t, (w_full, ids))
+    x_rel = jnp.concatenate(tie(x_pieces, a_t), axis=0).reshape(members, tok_rows, D)
 
     h2, gates, y1, h2_own, gates_own = mix_forward(
         pos, a_pieces, x_rel, w_full, gain_moe, weights, ids
     )
 
     give, keep, ag, dgu, dg = expert_main(pos, h2, dy_all, gates, w_gate_up, w_down)
-    dg = exchange(dg, "expert")[:, :EXP_DEV].reshape(expert_total, tok_rows).T
-    dg = jnp.pad(dg, ((0, 0), (ROUTE, 128 - ROUTE - expert_total)))
-    got, from_x, from_y = scatter_sum(give, keep)
-
+    got = swap(give, 1)
     down_wgrad = down_grad(pos, ag, dy_all, groups)
     down_share = lax.psum_scatter(
         down_wgrad.reshape(groups * EXP_DEV * FF, -1), "dp", scatter_dimension=0, tiled=True
     ).astype(F32).reshape(EXP_DEV, FF, -1)
-    up_wgrad = up_grad(pos, h2, dgu, groups)
+    sums = pair_sums(keep, tie(got, down_wgrad))
+    came_sums = send_sums(sums)
+    dg = exchange(tie(dg, sums), "expert")[:, :EXP_DEV].reshape(expert_total, tok_rows).T
+    dg = jnp.pad(dg, ((0, 0), (ROUTE, 128 - ROUTE - expert_total)))
+    up_wgrad = up_grad(pos, *tie((h2, dgu), sums), groups)
     up_share = lax.psum_scatter(up_wgrad, "dp", scatter_dimension=1, tiled=True).astype(F32)
-
-    out_give, out_keep = combine(pos, ag, w_down)
-    out_got, out_x, out_y = scatter_sum(out_give, out_keep)
-    result = (
-        y1
-        + out_keep[0].astype(F32)
-        + out_got[0].astype(F32)
-        + out_x.astype(F32)
-        + out_y.astype(F32)
-    ).astype(BF)
-
-    dy1, db, da, router_wgrad, moe_gain_grad = middle(
-        pos, keep, got, from_x, from_y, y1, h2_own, gates_own, dg, grad_out, weights, gain_moe, w_full
+    out_give, out_keep = combine(pos, tie(ag, up_wgrad), w_down)
+    out_got = swap(out_give, 1)
+
+    dy1, da, router_wgrad, moe_gain_grad = middle(
+        groups, pos, tie(keep, out_keep), got, came_sums, y1, h2_own, gates_own, dg, grad_out,
+        weights, gain_moe, w_full,
     )
     da = exchange(da, "expert")
-
-    db_cols = exchange(
-        jnp.moveaxis(db.reshape(tok_rows, groups, members, out_cols), 2, 0).reshape(
-            members, tok_rows, groups * out_cols
-        ),
-        "expert",
-    ).reshape(seq, groups * out_cols)
-    out_wgrad = out_grad(pos, a_pieces, db_cols).reshape(groups, out_cols, D)
-    out_share = jnp.sum(exchange(out_wgrad, "dp").astype(F32), axis=0).T
-
-    dq_t, dk_t, dv_t = attn_backward(first, q_t, da, o_t, lse, k, k_t, v, start)
-    give1, keep1, packed = back(pos, dq_t, dk_t, dv_t, cosine, sine, weights)
-    got1, from_x1, from_y1 = scatter_sum(give1, keep1)
-
-    sent = pack(pos, packed, x_rel, gain_attn, router_wgrad, moe_gain_grad)
+    out_sums = pair_sums(out_keep, tie(out_got, dy1))
+    out_came = send_sums(out_sums)
+
+    dq_t, dk_t, dv_t = attn_backward(first, q_t, tie(da, out_sums), o_t, lse, k, k_t, v, start)
+    result = y1 + out_keep[0].astype(F32) + out_got[0].astype(F32)
+    for term in out_came:
+        result = result + term.astype(F32)
+    result = result.astype(BF)
+    give1, keep1, packed = back(pos, tie(dq_t, result), dk_t, dv_t, cosine, sine, weights)
+    got1 = swap(give1, 1)
+    sent = pack(pos, packed, x_rel, gain_attn, weights, router_wgrad, moe_gain_grad)
+    sums1 = pair_sums(keep1, tie(got1, sent))
+    came_sums1 = send_sums(sums1)
+    sent = tie(sent, sums1)
+    out_wgrad = out_grad(pos, a_pieces, tie(da, sums1)).reshape(groups, out_cols, D)
+    out_terms = send_to_groups(out_wgrad)
     came = exchange(sent.reshape(devices, in_rows, PACK), BOTH)
     query_share, pair_share, rest = unpack(pos, came, groups)
     router_share = (
@@ -1011,11 +1042,9 @@
     )
     moe_gain_share = rest[:, ROUTE + 32] + rest[:, ROUTE + 33]
 
-    token_grad, attn_gain_grad = last(pos, keep1, got1, from_x1, from_y1, tokens, gain_attn, dy1)
-    gain_rows = jnp.pad(
-        attn_gain_grad[0].reshape(devices, in_rows), ((0, 0), (0, 128 - in_rows))
-    )
-    attn_gain_share = jnp.sum(exchange(gain_rows, BOTH), axis=0)[:in_rows]
+    attn_gain_share = rest[:, ROUTE + 34] + rest[:, ROUTE + 35]
+    token_grad = last(pos, keep1, got1, came_sums1, tie(tokens, rest), gain_attn, dy1)
+    out_share = sum(term.astype(F32) for term in tie(out_terms, token_grad)).T
 
     return (
         result,

time: 534 us -> 508 us (0.951)
  blocking collectives: 17 us -> 0 us
  Pallas kernels: 222 us -> 212 us
  other arithmetic: 35.3 us -> 29 us
  starting transfers between devices: 55.1 us -> 61.2 us
  waiting for transfers between devices: 139 us -> 145 us
    ppermute x33 -> x37, waiting for transfers between devices: 115 us -> 51.4 us  [swap(): return lax.ppermute(values, 'expert', [(i, i ^ bit) for i in range(count)])]
    all_gather x2, waiting for transfers between devices: 0.02 us -> 35.6 us  [the longest x1 23 us: shards(): w_full = lax.all_gather(tie(w_out.T, q_t), BOTH, axis=0, tiled=True)]
    all_to_all x7 -> x4, waiting for transfers between devices: 22.9 us -> 55.6 us  [exchange(): return lax.all_to_all(blocks, axes, split_axis=0, concat_axis=0, tiled=True)]
    all_to_all x1 -> x0, blocking collectives: 17 us -> none  [exchange(): return lax.all_to_all(blocks, axes, split_axis=0, concat_axis=0, tiled=True)]
    all_to_all x7 -> x4, starting transfers between devices: 30.8 us -> 18.3 us  [exchange(): return lax.all_to_all(blocks, axes, split_axis=0, concat_axis=0, tiled=True)]
    reduce_scatter x1, starting transfers between devices: 0.04 us -> 11.5 us  [shards(): lax.psum_scatter(down_wgrad.reshape(groups * EXP_DEV * FF, -1), 'dp', sca...]
    pallas_call x1, Pallas kernels: 28.9 us -> 21.4 us  [attn_backward(): pl.pallas_call(attn_bwd_kernel, grid_spec=pltpu.PrefetchScalarGridSpec(nu...]
    convert_element_type x3 -> x4, other arithmetic: 7.23 us -> 14.5 us  [the longest x3 11 us: pair_sums(): (keep[r].astype(F32) + got[r].astype(F32)).astype(BF)]
  transfers between devices with their start and end apart: 44 -> 48, of which waited for: 16 -> 11; matrix products, arithmetic and copies ran while one was open for 14% -> 11% of each run, Pallas kernels for 31% -> 31%
where the time goes in v1:
time: 508 us; the launch traced here: 504 us
  Pallas kernels  212 us (42%)
  waiting for transfers between devices  145 us (29%)
  starting transfers between devices  61.2 us (12%)
  local copies, waits for them, and re-layouts  42 us (8%)
  other arithmetic  29 us (6%)
  between operations  14.3 us (3%)
    all_to_all x4, waiting for transfers between devices, exchange(): return lax.all_to_all(blocks, axes, split_axis=0, concat_axis=0, tiled=True)  55.6 us
    ppermute x37, waiting for transfers between devices, swap(): return lax.ppermute(values, 'expert', [(i, i ^ bit) for i in range(count)])  51.4 us
    pallas_call x1, Pallas kernels, expert_main(): call(functools.partial(expert_kernel, half), 'experts', (steps,), [spec((...  44.6 us
    unnamed x74, local copies, waits for them, and re-layouts  27.4 us
    ppermute x37, starting transfers between devices, swap(): return lax.ppermute(values, 'expert', [(i, i ^ bit) for i in range(count)])  25.3 us
    pallas_call x1, Pallas kernels, mix_forward(): call(functools.partial(mix_kernel, count), 'mix', (seq // BLK,), [spec((a...  23.2 us
    all_gather x1, waiting for transfers between devices, shards(): w_full = lax.all_gather(tie(w_out.T, q_t), BOTH, axis=0, tiled=True)  23 us
    pallas_call x1, Pallas kernels, attn_backward(): pl.pallas_call(attn_bwd_kernel, grid_spec=pltpu.PrefetchScalarGridSpec(nu...  21.4 us
  transfers between devices with their start and end apart: 48, of which 11 were waited for; matrix products, arithmetic and copies ran while one was open for 11% of the time, Pallas kernels for 31%

profile of v1, /device:TPU:0, one launch (start us, length us, event | category | flops | bytes accessed | tf_op | source)
XLA Modules:
  0.0 504.0 jit_solution(9172813586696083056)
XLA Ops:
  12.4 7.3 %all-to-all-start = ((bf16[32,48,384]{2,1,0:T(8,128)(2,1)}), bf16[32,48,384]{2,1,0:T(8,128)(2,1)S(1)}, u32[]{:S(2)}, u32[]{:S(2)}) async-start(bf16[32,48,384]{2,1,0:T(8,128)(2,1)} %send_weights.1), calls=%async_computation | async-start | bytes 2359296 | tf_op jit(solution)/shard_map/all_to_all | solution.py:931
  23.1 29.0 %collective-permute-done.3.refs_4_ = bf16[256,1536]{1,0:T(8,128)(2,1)S(1)} collective-permute-done((bf16[256,1536]{1,0:T(8,128)(2,1)}, bf16[256,1536]{1,0:T(8,128)(2,1)S(1)}, u32[]{:S(2)}, u32[]{:S(2)}) %collective-permute-start.3) | collective-permute-done | bytes 786464 | tf_op jit(solution)/shard_map/ppermute | solution.py:889
  56.4 6.6 %collective-permute-done.6.refs_7_ = bf16[128,1536]{1,0:T(8,128)(2,1)} collective-permute-done((bf16[128,1536]{1,0:T(8,128)(2,1)S(1)}, bf16[128,1536]{1,0:T(8,128)(2,1)}, u32[]{:S(2)}, u32[]{:S(2)}) %collective-permute-start.6) | collective-permute-done | bytes 393248 | tf_op jit(solution)/shard_map/ppermute | solution.py:889
  69.9 9.1 %qkv.1 = (bf16[192,2048]{1,0:T(8,128)(2,1)}, bf16[64,2048]{1,0:T(8,128)(2,1)}, bf16[64,2048]{1,0:T(8,128)(2,1)}, bf16[2048,64]{1,0:T(8,128)(2,1)}, bf16[2048,64]{1,0:T(8,128)(2,1)}) custom-call(s32[1]{0:T(128)} %bitcast.pos_ref, bf16[256,1536]{1,0:T(8,128)(2,1)} %x_ref, bf16[256,1536]{1,0:T(8,128)(2,1)} %collective-permute-done.refs_1_, ...), custom_call_target="tpu_custom_call" | custom-call | flops 399999991808 | bytes 10000 | tf_op jit(solution)/shard_map/qkv/pallas_call | solution.py:317
  81.3 16.5 %attn_fwd.1 = (bf16[192,2048]{1,0:T(8,128)(2,1)}, f32[192,2048]{1,0:T(8,128)}, f32[8,2048]{1,0:T(8,128)}) custom-call(s32[8]{0:T(128)} %and_select_fusion.first_ref, bf16[192,2048]{1,0:T(8,128)(2,1)} %get-tuple-element.81.q_ref, bf16[2048,64]{1,0:T(8,128)(2,1)} %get-tuple-element.82.k_ref, bf16[64,2048]{1,0:T(8,128)(2,1)} %get-tuple-element.83.vt_ref, ...), custom_call_target="tpu_custom_call" | custom-call | flops 49999998976 | bytes 10000 | tf_op jit(solution)/shard_map/attn_fwd/pallas_call | solution.py:157
  128.0 23.0 %all-gather.3.cloned.1.call-done = bf16[1536,1536]{1,0:T(8,128)(2,1)} async-done(((bf16[48,1536]{1,0:T(8,128)(2,1)}), bf16[1536,1536]{1,0:T(8,128)(2,1)}) %all-gather.3.cloned.1.call-update) | async-done | bytes 4718608 | tf_op jit(solution)/shard_map/all_gather | solution.py:988
  151.0 6.6 %copy.43 = bf16[1536,1536]{0,1:T(8,128)(2,1)} copy(bf16[1536,1536]{1,0:T(8,128)(2,1)} %all-gather.3.cloned.1.call-done) | data formatting | bytes 9437184 | tf_op jit(solution)/shard_map/all_gather | solution.py:988
  163.4 23.2 %mix.1 = (bf16[2048,1536]{1,0:T(8,128)(2,1)}, f32[2048,128]{1,0:T(8,128)}, f32[256,1536]{1,0:T(8,128)}, bf16[256,1536]{1,0:T(8,128)(2,1)}, f32[256,128]{1,0:T(8,128)}) custom-call(s32[1]{0:T(128)} %bitcast.pos_ref, bf16[192,2048]{1,0:T(8,128)(2,1)} %get-tuple-element.84.refs_0_, bf16[192,2048]{1,0:T(8,128)(2,1)} %copy-done.14, bf16[192,2048]{1,0:T(8,128)(2,1)} %copy-done.6, ...), custom_call_target="tpu_custom_call" | custom-call | flops 49999998976 | bytes 10000 | tf_op jit(solution)/shard_map/mix/pallas_call | solution.py:401
  186.6 12.6 %all-gather.5.cloned.1.call-done.dy_ref = bf16[2048,1536]{1,0:T(8,128)(2,1)} async-done(((bf16[256,1536]{1,0:T(8,128)(2,1)}), bf16[2048,1536]{1,0:T(8,128)(2,1)}) %all-gather.5.cloned.1.call-update) | async-done | bytes 6291472 | tf_op jit(solution)/shard_map/all_gather | solution.py:989
  199.2 44.6 %experts.1 = (bf16[4,256,1536]{2,1,0:T(8,128)(2,1)}, bf16[4,256,1536]{2,1,0:T(8,128)(2,1)}, bf16[2,2048,512]{2,1,0:T(8,128)(2,1)}, bf16[2,2048,1024]{2,1,0:T(8,128)(2,1)}, f32[8,8,256]{2,1,0:T(8,128)}) custom-call(s32[1]{0:T(128)} %bitcast.pos_ref, bf16[2048,1536]{1,0:T(8,128)(2,1)} %get-tuple-element.108.h2_ref, ...), custom_call_target="tpu_custom_call" | custom-call | flops 49999998976 | bytes 10000 | tf_op jit(solution)/shard_map/experts/pallas_call | solution.py:477
  244.1 14.8 %down_grad.1 = bf16[4,2,512,384]{3,2,1,0:T(8,128)(2,1)} custom-call(s32[1]{0:T(128)} %bitcast.pos_ref, bf16[2,2048,512]{2,1,0:T(8,128)(2,1)} %get-tuple-element.110.ag_ref, bf16[2048,1536]{1,0:T(8,128)(2,1)} %all-gather.5.cloned.1.call-done.dy_ref), custom_call_target="tpu_custom_call" | custom-call | bytes 10000 | tf_op jit(solution)/shard_map/down_grad/pallas_call | solution.py:514
  269.1 11.5 %reduce-scatter.5.cloned.1.call-start = ((), (), s32[]{:S(2)}) async-start(), calls=%async_computation.9 | async-start | bytes 3932160 | tf_op jit(solution)/shard_map/reduce_scatter | solution.py:1004
  280.6 19.5 %up_grad.1 = bf16[2,1536,1024]{2,1,0:T(8,128)(2,1)} custom-call(s32[1]{0:T(128)} %bitcast.pos_ref, bf16[2048,1536]{1,0:T(8,128)(2,1)} %get-tuple-element.108.h2_ref, bf16[2,2048,1024]{2,1,0:T(8,128)(2,1)} %get-tuple-element.109.dgu_ref), custom_call_target="tpu_custom_call" | custom-call | bytes 10000 | tf_op jit(solution)/shard_map/up_grad/pallas_call | solution.py:538
  300.1 12.6 %combine.1 = (bf16[4,256,1536]{2,1,0:T(8,128)(2,1)}, bf16[4,256,1536]{2,1,0:T(8,128)(2,1)}) custom-call(s32[1]{0:T(128)} %bitcast.pos_ref, bf16[2,2048,512]{2,1,0:T(8,128)(2,1)} %get-tuple-element.110.ag_ref, bf16[2,512,1536]{2,1,0:T(8,128)(2,1)} %down_ref.3), custom_call_target="tpu_custom_call" | custom-call | bytes 10000 | tf_op jit(solution)/shard_map/combine/pallas_call | solution.py:572
  315.2 8.8 %middle.1 = (f32[256,1536]{1,0:T(8,128)}, bf16[256,1536]{1,0:T(8,128)(2,1)}, bf16[8,384,256]{2,1,0:T(8,128)(2,1)}, f32[1536,128]{1,0:T(8,128)}, f32[8,1536]{1,0:T(8,128)}) custom-call(s32[1]{0:T(128)} %bitcast.pos_ref, bf16[4,256,1536]{2,1,0:T(8,128)(2,1)} %get-tuple-element.113.keep_ref, bf16[4,256,1536]{2,1,0:T(8,128)(2,1)} %collective-permute-done.25.got_ref, ...), custom_call_target="tpu_custom_call" | custom-call | flops 99999997952 | bytes 10000 | tf_op jit(solution)/shard_map/middle/pallas_call | solution.py:638
  328.4 4.2 fusion.7
  336.1 13.3 %all-to-all-done.2.da_ref.refs_10_ = bf16[8,384,256]{2,1,0:T(8,128)(2,1)S(1)} async-done(((bf16[8,384,256]{2,1,0:T(8,128)(2,1)}), bf16[8,384,256]{2,1,0:T(8,128)(2,1)S(1)}, u32[]{:S(2)}, u32[]{:S(2)}) %all-to-all-start.2) | async-done | bytes 1572896 | tf_op jit(solution)/shard_map/all_to_all | solution.py:931
  350.6 21.4 %attn_bwd.1 = (f32[192,2048]{1,0:T(8,128)}, f32[64,2048]{1,0:T(8,128)}, f32[64,2048]{1,0:T(8,128)}) custom-call(s32[8]{0:T(128)} %and_select_fusion.first_ref, bf16[192,2048]{1,0:T(8,128)(2,1)} %get-tuple-element.81.q_ref, bf16[8,384,256]{2,1,0:T(8,128)(2,1)} %copy-done.1, f32[192,2048]{1,0:T(8,128)} %get-tuple-element.122.o_ref, ...), custom_call_target="tpu_custom_call" | custom-call | flops 20000000000 | bytes 10000 | tf_op jit(solution)/shard_map/attn_bwd/pallas_call | solution.py:189
  372.1 10.7 %collective-permute-done.32 = bf16[256,1536]{1,0:T(8,128)(2,1)} collective-permute-done((bf16[256,1536]{1,0:T(8,128)(2,1)}, bf16[256,1536]{1,0:T(8,128)(2,1)}, u32[]{:S(2)}, u32[]{:S(2)}) %collective-permute-start.32) | collective-permute-done | bytes 786464 | tf_op jit(solution)/shard_map/ppermute | solution.py:889
  386.3 10.5 %back.1 = (bf16[4,256,1536]{2,1,0:T(8,128)(2,1)}, bf16[4,256,1536]{2,1,0:T(8,128)(2,1)}, bf16[384,2048]{1,0:T(8,128)(2,1)}) custom-call(s32[1]{0:T(128)} %bitcast.pos_ref, f32[192,2048]{1,0:T(8,128)} %get-tuple-element.127.dq_ref, f32[64,2048]{1,0:T(8,128)} %get-tuple-element.128.dk_ref, f32[64,2048]{1,0:T(8,128)} %get-tuple-element.129.dv_ref, ...), custom_call_target="tpu_custom_call" | custom-call | flops 10000000000 | bytes 10000 | tf_op jit(solution)/shard_map/back/pallas_call | solution.py:703
  396.8 12.7 %pack.1 = bf16[1536,384]{1,0:T(8,128)(2,1)} custom-call(s32[1]{0:T(128)} %bitcast.pos_ref, bf16[384,2048]{1,0:T(8,128)(2,1)} %get-tuple-element.132.packed_ref, bf16[8,256,1536]{2,1,0:T(8,128)(2,1)} %bitcast.10.refs_10_.x_ref, f32[1,1536]{1,0:T(1,128)} %reshape.138.refs_11_.gain_ref, bf16[1536,384]{1,0:T(8,128)(2,1)} %bitcast.67, ...), custom_call_target="tpu_custom_call" | custom-call | bytes 10000 | tf_op jit(solution)/shard_map/pack/pallas_call | solution.py:765
  422.7 9.0 %out_grad.1 = f32[192,1536]{1,0:T(8,128)} custom-call(s32[1]{0:T(128)} %bitcast.pos_ref, bf16[192,2048]{1,0:T(8,128)(2,1)} %get-tuple-element.84.refs_0_, bf16[192,2048]{1,0:T(8,128)(2,1)} %copy-done.14, bf16[192,2048]{1,0:T(8,128)(2,1)} %copy-done.6, bf16[192,2048]{1,0:T(8,128)(2,1)} %collective-permute-done.11.refs_3_, bf16[192,2048]{1,0:T(8,128)(2,1)} %copy-done.5, ...), custom_call_target="tpu_custom_call" | custom-call | bytes 10000 | tf_op jit(solution)/shard_map/out_grad/pallas_call | solution.py:841
  436.7 42.2 %all-to-all-done.3.came_ref = bf16[32,48,384]{2,1,0:T(8,128)(2,1)S(1)} async-done(((bf16[32,48,384]{2,1,0:T(8,128)(2,1)}), bf16[32,48,384]{2,1,0:T(8,128)(2,1)S(1)}, u32[]{:S(2)}, u32[]{:S(2)}) %all-to-all-start.3) | async-done | bytes 1179680 | tf_op jit(solution)/shard_map/all_to_all | solution.py:931
  484.2 5.1 %last.1 = bf16[256,1536]{1,0:T(8,128)(2,1)} custom-call(s32[1]{0:T(128)} %bitcast.pos_ref, bf16[4,256,1536]{2,1,0:T(8,128)(2,1)} %get-tuple-element.130.keep_ref, bf16[4,256,1536]{2,1,0:T(8,128)(2,1)} %collective-permute-done.33.got_ref, bf16[256,1536]{1,0:T(8,128)(2,1)} %collective-permute-done.34.fx_ref, bf16[256,1536]{1,0:T(8,128)(2,1)} %collective-permute-done.35.fy_ref, ...), custom_call_target="tpu_custom_call" | custom-call | flops 49999998976 | bytes 10000 | tf_op jit(solution)/shard_map/last/pallas_call | solution.py:802
  (201 shorter events, 114.9 us)
Async XLA Ops:
  12.4 55.0 %all-to-all-start = ((bf16[32,48,384]{2,1,0:T(8,128)(2,1)}), bf16[32,48,384]{2,1,0:T(8,128)(2,1)S(1)}, u32[]{:S(2)}, u32[]{:S(2)}) async-start(bf16[32,48,384]{2,1,0:T(8,128)(2,1)} %send_weights.1), calls=%async_computation | async-start | bytes 2359296 | tf_op jit(solution)/shard_map/all_to_all | solution.py:931
  19.7 131.3 %all-gather.3.cloned.1.call-start = ((), (), s32[]{:S(2)}) async-start(), calls=%async_computation.6 | async-start | bytes 4866048 | tf_op jit(solution)/shard_map/all_gather | solution.py:988
  23.0 46.0 %collective-permute-start = (bf16[256,1536]{1,0:T(8,128)(2,1)}, bf16[256,1536]{1,0:T(8,128)(2,1)}, u32[]{:S(2)}, u32[]{:S(2)}) collective-permute-start(bf16[256,1536]{1,0:T(8,128)(2,1)} %x_ref), channel_id=1, source_target_pairs={{0,1},{1,0},{2,3},{3,2},{4,5},{5,4},{6,7},{7,6},{8,9},{9,8},{10,11... | collective-permute-start | bytes 2359304 | tf_op jit(solution)/shard_map/ppermute | solution.py:889
  79.1 120.1 %all-gather.5.cloned.1.call-start = ((), (), s32[]{:S(2)}) async-start(), calls=%async_computation.7 | async-start | bytes 7077888 | tf_op jit(solution)/shard_map/all_gather | solution.py:989
  79.4 37.5 %collective-permute-start.21 = (s32[8,256]{1,0:T(8,128)S(1)}, s32[8,256]{1,0:T(8,128)S(1)}, u32[]{:S(2)}, u32[]{:S(2)}) collective-permute-start(s32[8,256]{1,0:T(8,128)S(1)} %bitcast.74), channel_id=1, source_target_pairs={{0,6},{1,7},{2,4},{3,5},{4,2},{5,3},{6,0},{7,1},{8,14},{9,15},{10,... | collective-permute-start | bytes 24584 | tf_op jit(solution)/shard_map/ppermute | solution.py:889
  116.9 44.9 %collective-permute-start.9 = (bf16[192,2048]{1,0:T(8,128)(2,1)S(1)}, bf16[192,2048]{1,0:T(8,128)(2,1)S(1)}, u32[]{:S(2)}, u32[]{:S(2)}) collective-permute-start(bf16[192,2048]{1,0:T(8,128)(2,1)S(1)} %copy-done.13), channel_id=1, source_target_pairs={{0,1},{1,0},{2,3},{3,2},{4,5},{5,4},{6,7},{7,6},{8,9},{9,8},{10,11... | collective-permute-start | bytes 2359304 | tf_op jit(solution)/shard_map/ppermute | solution.py:889
  122.3 35.4 %collective-permute-start.15 = (bf16[96,2048]{1,0:T(8,128)(2,1)}, bf16[96,2048]{1,0:T(8,128)(2,1)S(1)}, u32[]{:S(2)}, u32[]{:S(2)}) collective-permute-start(bf16[96,2048]{1,0:T(8,128)(2,1)} %slice.140), channel_id=1, source_target_pairs={{0,2},{1,3},{2,0},{3,1},{4,6},{5,7},{6,4},{7,5},{8,10},{9,11},{10,... | collective-permute-start | bytes 1179656 | tf_op jit(solution)/shard_map/ppermute | solution.py:889
  125.7 36.2 %collective-permute-start.13 = (bf16[192,2048]{1,0:T(8,128)(2,1)S(1)}, bf16[192,2048]{1,0:T(8,128)(2,1)}, u32[]{:S(2)}, u32[]{:S(2)}) collective-permute-start(bf16[192,2048]{1,0:T(8,128)(2,1)S(1)} %collective-permute-done.12.refs_4_), channel_id=1, source_target_pairs={{0,1},{1,0},{2,3},{3,2},{4,5},{5,4},{6,7},{7,6},{8,9},{9,8},{10,11... | collective-permute-start | bytes 2359304 | tf_op jit(solution)/shard_map/ppermute | solution.py:889
  125.7 36.1 %collective-permute-start.11 = (bf16[192,2048]{1,0:T(8,128)(2,1)S(1)}, bf16[192,2048]{1,0:T(8,128)(2,1)}, u32[]{:S(2)}, u32[]{:S(2)}) collective-permute-start(bf16[192,2048]{1,0:T(8,128)(2,1)S(1)} %collective-permute-done.10.refs_2_), channel_id=1, source_target_pairs={{0,1},{1,0},{2,3},{3,2},{4,5},{5,4},{6,7},{7,6},{8,9},{9,8},{10,11... | collective-permute-start | bytes 2359304 | tf_op jit(solution)/shard_map/ppermute | solution.py:889
  262.2 51.5 %collective-permute-start.29 = (bf16[256,1536]{1,0:T(8,128)(2,1)}, bf16[256,1536]{1,0:T(8,128)(2,1)S(1)}, u32[]{:S(2)}, u32[]{:S(2)}) collective-permute-start(bf16[256,1536]{1,0:T(8,128)(2,1)} %get-tuple-element.196), channel_id=1, source_target_pairs={{0,6},{1,7},{2,4},{3,5},{4,2},{5,3},{6,0},{7,1},{8,14},{9,15},{10,... | collective-permute-start | bytes 2359304 | tf_op jit(solution)/shard_map/ppermute | solution.py:889
  263.6 50.2 %collective-permute-start.28 = (bf16[256,1536]{1,0:T(8,128)(2,1)}, bf16[256,1536]{1,0:T(8,128)(2,1)S(1)}, u32[]{:S(2)}, u32[]{:S(2)}) collective-permute-start(bf16[256,1536]{1,0:T(8,128)(2,1)} %get-tuple-element.197), channel_id=1, source_target_pairs={{0,4},{1,5},{2,6},{3,7},{4,0},{5,1},{6,2},{7,3},{8,12},{9,13},{10,... | collective-permute-start | bytes 2359304 | tf_op jit(solution)/shard_map/ppermute | solution.py:889
  265.1 48.6 %collective-permute-start.27 = (bf16[256,1536]{1,0:T(8,128)(2,1)}, bf16[256,1536]{1,0:T(8,128)(2,1)S(1)}, u32[]{:S(2)}, u32[]{:S(2)}) collective-permute-start(bf16[256,1536]{1,0:T(8,128)(2,1)} %get-tuple-element.198), channel_id=1, source_target_pairs={{0,2},{1,3},{2,0},{3,1},{4,6},{5,7},{6,4},{7,5},{8,10},{9,11},{10,... | collective-permute-start | bytes 2359304 | tf_op jit(solution)/shard_map/ppermute | solution.py:889
  265.7 47.2 %all-to-all-start.1 = ((f32[8,8,256]{2,1,0:T(8,128)}), f32[8,8,256]{2,1,0:T(8,128)S(1)}, u32[]{:S(2)}, u32[]{:S(2)}) async-start(f32[8,8,256]{2,1,0:T(8,128)} %get-tuple-element.117), calls=%async_computation.1 | async-start | bytes 131072 | tf_op jit(solution)/shard_map/all_to_all | solution.py:931
  269.1 151.2 %reduce-scatter.5.cloned.1.call-start = ((), (), s32[]{:S(2)}) async-start(), calls=%async_computation.9 | async-start | bytes 3932160 | tf_op jit(solution)/shard_map/reduce_scatter | solution.py:1004
  327.8 166.0 %reduce-scatter.3.cloned.1.call-start = ((), (), s32[]{:S(2)}) async-start(), calls=%async_computation.8 | async-start | bytes 7864320 | tf_op jit(solution)/shard_map/reduce_scatter | solution.py:1012
  332.6 39.5 %collective-permute-start.30 = (bf16[256,1536]{1,0:T(8,128)(2,1)}, bf16[256,1536]{1,0:T(8,128)(2,1)}, u32[]{:S(2)}, u32[]{:S(2)}) collective-permute-start(bf16[256,1536]{1,0:T(8,128)(2,1)} %get-tuple-element.193), channel_id=1, source_target_pairs={{0,2},{1,3},{2,0},{3,1},{4,6},{5,7},{6,4},{7,5},{8,10},{9,11},{10,... | collective-permute-start | bytes 2359304 | tf_op jit(solution)/shard_map/ppermute | solution.py:889
  334.5 48.2 %collective-permute-start.32 = (bf16[256,1536]{1,0:T(8,128)(2,1)}, bf16[256,1536]{1,0:T(8,128)(2,1)}, u32[]{:S(2)}, u32[]{:S(2)}) collective-permute-start(bf16[256,1536]{1,0:T(8,128)(2,1)} %get-tuple-element.194), channel_id=1, source_target_pairs={{0,6},{1,7},{2,4},{3,5},{4,2},{5,3},{6,0},{7,1},{8,14},{9,15},{10,... | collective-permute-start | bytes 2359304 | tf_op jit(solution)/shard_map/ppermute | solution.py:889
  336.0 46.7 %collective-permute-start.31 = (bf16[256,1536]{1,0:T(8,128)(2,1)}, bf16[256,1536]{1,0:T(8,128)(2,1)}, u32[]{:S(2)}, u32[]{:S(2)}) collective-permute-start(bf16[256,1536]{1,0:T(8,128)(2,1)} %get-tuple-element.195), channel_id=1, source_target_pairs={{0,4},{1,5},{2,6},{3,7},{4,0},{5,1},{6,2},{7,3},{8,12},{9,13},{10,... | collective-permute-start | bytes 2359304 | tf_op jit(solution)/shard_map/ppermute | solution.py:889
  412.9 66.0 %all-to-all-start.3 = ((bf16[32,48,384]{2,1,0:T(8,128)(2,1)}), bf16[32,48,384]{2,1,0:T(8,128)(2,1)S(1)}, u32[]{:S(2)}, u32[]{:S(2)}) async-start(bf16[32,48,384]{2,1,0:T(8,128)(2,1)} %bitcast.23), calls=%async_computation.3 | async-start | bytes 2359296 | tf_op jit(solution)/shard_map/all_to_all | solution.py:931
  416.7 65.5 %collective-permute-start.36 = (bf16[256,1536]{1,0:T(8,128)(2,1)}, bf16[256,1536]{1,0:T(8,128)(2,1)S(1)}, u32[]{:S(2)}, u32[]{:S(2)}) collective-permute-start(bf16[256,1536]{1,0:T(8,128)(2,1)} %get-tuple-element.190), channel_id=1, source_target_pairs={{0,6},{1,7},{2,4},{3,5},{4,2},{5,3},{6,0},{7,1},{8,14},{9,15},{10,... | collective-permute-start | bytes 2359304 | tf_op jit(solution)/shard_map/ppermute | solution.py:889
  419.5 64.7 %collective-permute-start.35 = (bf16[256,1536]{1,0:T(8,128)(2,1)}, bf16[256,1536]{1,0:T(8,128)(2,1)}, u32[]{:S(2)}, u32[]{:S(2)}) collective-permute-start(bf16[256,1536]{1,0:T(8,128)(2,1)} %get-tuple-element.191), channel_id=1, source_target_pairs={{0,4},{1,5},{2,6},{3,7},{4,0},{5,1},{6,2},{7,3},{8,12},{9,13},{10,... | collective-permute-start | bytes 2359304 | tf_op jit(solution)/shard_map/ppermute | solution.py:889
  420.0 64.1 %collective-permute-start.34 = (bf16[256,1536]{1,0:T(8,128)(2,1)}, bf16[256,1536]{1,0:T(8,128)(2,1)}, u32[]{:S(2)}, u32[]{:S(2)}) collective-permute-start(bf16[256,1536]{1,0:T(8,128)(2,1)} %get-tuple-element.192), channel_id=1, source_target_pairs={{0,2},{1,3},{2,0},{3,1},{4,6},{5,7},{6,4},{7,5},{8,10},{9,11},{10,... | collective-permute-start | bytes 2359304 | tf_op jit(solution)/shard_map/ppermute | solution.py:889
  433.0 57.0 %collective-permute-start.39 = (bf16[48,1536]{1,0:T(8,128)(2,1)S(1)}, bf16[48,1536]{1,0:T(8,128)(2,1)S(1)}, u32[]{:S(2)}, u32[]{:S(2)}) collective-permute-start(bf16[48,1536]{1,0:T(8,128)(2,1)S(1)} %get-tuple-element.199), channel_id=1, source_target_pairs={{0,24},{8,0},{16,8},{24,16},{1,25},{9,1},{17,9},{25,17},{2,26},{10... | collective-permute-start | bytes 442376 | tf_op jit(solution)/shard_map/ppermute | solution.py:926
  436.7 55.6 %collective-permute-start.38 = (bf16[48,1536]{1,0:T(8,128)(2,1)S(1)}, bf16[48,1536]{1,0:T(8,128)(2,1)S(1)}, u32[]{:S(2)}, u32[]{:S(2)}) collective-permute-start(bf16[48,1536]{1,0:T(8,128)(2,1)S(1)} %get-tuple-element.200), channel_id=1, source_target_pairs={{0,16},{8,24},{16,0},{24,8},{1,17},{9,25},{17,1},{25,9},{2,18},{10... | collective-permute-start | bytes 442376 | tf_op jit(solution)/shard_map/ppermute | solution.py:926
  (52 other events, 688.9 us)
Sparse Core Ops, SparseCore 0:
  79.2 71.7 all-gather.2
  152.9 46.2 all-gather.4
  280.7 61.3 reduce-scatter.4
  344.3 134.3 reduce-scatter.2
